TPU v7x, 32 devices: a whole 2x2x4 slice. The times are simulated.
32 devices in a mesh: row: 4 (over y, x), col: 8 (over z, core).
Axes of the slice: x: 2, y: 2, z: 4, core: 2. Of those that a mesh axis runs over, the one named last changes fastest.
Arguments:
- trail: float32 [2, 4, 512, 2, 8, 512], P(None, 'row', None, None, 'col'), may hold values from -6 to 6
- panel: float32 [2, 4, 512, 512], P(None, 'row', None, 'col'), may hold values from -6 to 6
- row_basis: float32 [2, 4, 64, 512], P(None, 'row', None, 'col'), may hold values from -0.75 to 0.75
- row_coeff: float32 [2, 4, 64, 512], P(None, 'row', None, 'col'), may hold values from -0.25 to 0.25
- col_basis: float32 [2, 8, 64, 512], P(None, 'col', None, 'row'), may hold values from -0.75 to 0.75
- col_scaled: float32 [2, 8, 64, 512], P(None, 'col', None, 'row'), may hold values from -0.25 to 0.25
- pivot_basis: float32 [64, 512], P(None, 'col'), may hold values from -0.75 to 0.75
- pivot_scaled: float32 [64, 512], replicated, may hold values from -0.25 to 0.25
- sketch: float32 [64, 512], replicated, may hold values from -6 to 6
- perm: int32 [512], replicated, may hold values from 0 to 511, each once
- pair_kind: int32 [256], replicated, may hold values from 0 to 1
- pivot_values: float32 [3, 256], replicated, may hold values from -3 to 3, as said below
Outputs:
- trail_out: float32 [2, 4, 512, 2, 8, 512], P(None, 'row', None, None, 'col')
- basis_out: float32 [2, 4, 64, 512], P(None, 'row')
- coeff_out: float32 [2, 4, 64, 512], P(None, 'row')
Inputs may be any that keep to these rules, and one draw needn't show every extreme that they name: `pivot_values`: rows 0 and 1 have magnitudes between 0.5 and 0.7; row 2 has magnitude 1.2 or more.
All inputs are finite; a program needn't handle non-finite values.
Results may differ from a plain program's by a relative error of at most 0.00013.
Values sent between devices are 32-bit elements; how exact they have to be, the bound alone decides.
No kernel may reach another device: no remote copies, remote signals or barrier semaphores. Data moves between devices by JAX's collectives and lax.ppermute only.
A program may use at most 64 MiB of HBM per device.

v0:
```python
import jax
import jax.numpy as jnp
from jax import lax
from jax.experimental import pallas as pl
from jax.experimental.pallas import tpu as pltpu
from jax.sharding import PartitionSpec as P


F32 = jnp.float32
BF16 = jnp.bfloat16
HIGHEST = lax.Precision.HIGHEST


def dot_nn(left, right):
    return lax.dot_general(
        left, right, (((1,), (0,)), ((), ())), precision=HIGHEST, preferred_element_type=F32
    )


def dot_nt(left, right):
    return lax.dot_general(
        left, right, (((1,), (1,)), ((), ())), precision=HIGHEST, preferred_element_type=F32
    )


def split3(x):
    high = x.astype(BF16)
    rest = x - high.astype(F32)
    mid = rest.astype(BF16)
    low = (rest - mid.astype(F32)).astype(BF16)
    return high, mid, low


def onehot_dot(x, onehot, dims):
    rows = x.shape[0]
    parts = lax.dot_general(
        jnp.concatenate(split3(x), axis=0),
        onehot,
        (dims, ((), ())),
        preferred_element_type=F32,
    )
    return parts[:rows] + (parts[rows : 2 * rows] + parts[2 * rows :])


def call(kernel, outs, *args, fetched=0, kept=0, scratch=(), flops=0):
    vmem = pl.BlockSpec(memory_space=pltpu.VMEM)
    hbm = pl.BlockSpec(memory_space=pltpu.HBM)
    many = isinstance(outs, (list, tuple))
    args = [
        pltpu.with_memory_space_constraint(x, pltpu.HBM) if n < fetched + kept else x
        for n, x in enumerate(args)
    ]
    buffers = [pltpu.VMEM(x.shape, x.dtype) for x in args[:fetched]]

    def wrapped(*refs):
        refs = list(refs)
        extra = refs[len(refs) - fetched - 1 :] if fetched else []
        if fetched:
            refs = refs[: len(refs) - fetched - 1]
            copies = [
                pltpu.make_async_copy(refs[n], extra[n], extra[-1].at[n]) for n in range(fetched)
            ]
            for copy in copies:
                copy.start()
            for copy in copies:
                copy.wait()
            refs[:fetched] = extra[:fetched]
        kernel(*refs)

    scratch = list(scratch)
    if fetched:
        scratch += buffers + [pltpu.SemaphoreType.DMA((fetched,))]
    return pl.pallas_call(
        wrapped,
        out_shape=outs,
        in_specs=[hbm] * (fetched + kept) + [vmem] * (len(args) - fetched - kept),
        out_specs=[vmem] * len(outs) if many else vmem,
        scratch_shapes=scratch,
        cost_estimate=pl.CostEstimate(flops=flops, transcendentals=0, bytes_accessed=1 << 20),
        compiler_params=pltpu.CompilerParams(vmem_limit_bytes=8 << 20),
    )(*args)


def shape(*dims):
    return jax.ShapeDtypeStruct(dims, F32)


def pair_scale(rows, diag, off):
    length = rows.shape[1]
    lane = lax.broadcasted_iota(jnp.int32, rows.shape, 1)
    after = pltpu.roll(rows, length - 1, 1)
    before = pltpu.roll(rows, 1, 1)
    return rows * diag + jnp.where(lane % 2 == 0, after, before) * off


def selector_of(perm):
    length = perm.shape[1]
    row = lax.broadcasted_iota(jnp.int32, (length, length), 0)
    return (row == perm).astype(F32).astype(BF16)


def sketch_kernel(sketch_ref, perm_ref, kind_ref, values_ref, out_ref, coef_ref):
    pairs = kind_ref.shape[1]
    length = perm_ref.shape[1]
    one, two, cross = values_ref[0:1, :], values_ref[1:2, :], values_ref[2:3, :]
    twin = kind_ref[...] == 1
    det = one * two - cross * cross
    first = jnp.where(twin, two / det, 1.0 / one)
    second = jnp.where(twin, one / det, 1.0 / two)
    mixed = jnp.where(twin, -cross / det, 0.0)
    row = lax.broadcasted_iota(jnp.int32, (16, pairs), 0)
    stacked = jnp.where(row == 0, first, jnp.where(row == 1, second, mixed))
    pair = lax.broadcasted_iota(jnp.int32, (pairs, length), 0)
    lane = lax.broadcasted_iota(jnp.int32, (pairs, length), 1)
    even = (lane == 2 * pair).astype(F32).astype(BF16)
    odd = (lane == 2 * pair + 1).astype(F32).astype(BF16)
    at_even = onehot_dot(stacked, even, ((1,), (0,)))
    at_odd = onehot_dot(stacked, odd, ((1,), (0,)))
    diag = at_even[0:1] + at_odd[1:2]
    off = at_even[2:3] + at_odd[2:3]
    coef_ref[0:1, :] = diag
    coef_ref[1:2, :] = off
    scaled = pair_scale(sketch_ref[...], diag, off)
    placed = onehot_dot(scaled, selector_of(perm_ref[...]), ((1,), (1,)))
    chips, _, width = out_ref.shape
    for chip in range(chips):
        out_ref[chip] = placed[:, chip * width : (chip + 1) * width]


def stages(size):
    bits = []
    bit = size // 2
    while bit:
        bits.append(bit)
        bit //= 2
    return bits


def codes(size):
    order = [0]
    for bit in stages(size):
        order = order + [code ^ bit for code in order]
    return order


def stack_kernel(*refs):
    piece_refs, out_ref = refs[:-1], refs[-1]
    at = 0
    for piece_ref in piece_refs:
        out_ref[at : at + piece_ref.shape[0]] = piece_ref[...]
        at += piece_ref.shape[0]


def stack(*pieces):
    total = sum(piece.shape[0] for piece in pieces)
    return call(stack_kernel, shape(total, *pieces[0].shape[1:]), *pieces)


def gather(x, size, send):
    pieces = [x]
    for bit in stages(size):
        held = pieces[0] if len(pieces) == 1 else stack(*pieces)
        pieces = [held, send(held, bit)]
    return pieces


def entries(refs, size):
    order = codes(size)
    at = 0
    for ref in refs:
        for t in range(ref.shape[0]):
            yield order[at], ref, t
            at += 1


def lanes(ref, *index):
    low, high = index[-2:]
    lead = index[:-2]
    return jnp.concatenate(
        [ref[(chip, *lead, slice(low, high))] for chip in range(ref.shape[0])], axis=1
    )


def load_kernel(*refs):
    count = (len(refs) - 13) // 2
    packed, sources, (out_ref, cols_ref) = refs[:5], refs[5 : 5 + count], refs[5 + count : 7 + count]
    targets, buffers, sems = refs[7 + count : 7 + 2 * count], refs[7 + 2 * count : -1], refs[-1]
    core = lax.axis_index("col") % 2
    pairs = list(zip(packed, buffers))
    for source, target in zip(sources, targets):
        pairs.append((source.at[core] if len(source.shape) == 3 else source, target))
    copies = [
        pltpu.make_async_copy(source, target, sems.at[n])
        for n, (source, target) in enumerate(pairs)
    ]
    for copy in copies:
        copy.start()
    for copy in copies[:5]:
        copy.wait()
    row_basis_ref, row_coeff_ref, pivot_ref, col_basis_ref, col_scaled_ref = buffers
    rank = row_basis_ref.shape[1]
    half = rank // 2
    part = row_basis_ref.shape[2]
    for tile in range(2):
        where = slice(tile * part, (tile + 1) * part)
        out_ref[0, :rank, where] = row_basis_ref[tile]
        out_ref[0, rank : 2 * rank, where] = row_coeff_ref[tile]
        out_ref[0, 2 * rank :, where] = pivot_ref[tile * half : (tile + 1) * half]
    for col in range(col_basis_ref.shape[0]):
        base = 2 * col * rank
        cols_ref[0, base : base + rank] = col_basis_ref[col]
        cols_ref[0, base + rank : base + 2 * rank] = col_scaled_ref[col]
    for copy in copies[5:]:
        copy.wait()


def partial_kernel(sketch_ref, own_ref, other_ref, out_ref, panel_ref):
    core = lax.axis_index("col") % 2
    chip = lax.axis_index("col") // 2
    part = own_ref.shape[0]
    panel_ref[pl.ds(pl.multiple_of(core * part, part), part), :] = own_ref[...]
    panel_ref[pl.ds(pl.multiple_of((1 - core) * part, part), part), :] = other_ref[core]
    out_ref[...] = dot_nn(sketch_ref[chip], panel_ref[...])


def add_kernel(left_ref, right_ref, out_ref):
    out_ref[...] = left_ref[...] + right_ref[...]


def prepare_kernel(chips, pivot_ref, *refs):
    count = (len(refs) - 5) // 2
    own_refs, other_refs = refs[:count], refs[count : 2 * count]
    sketch_ref, panel_ref, factors_ref, corr_ref, updated_ref = refs[2 * count :]
    core = lax.axis_index("col") % 2
    chip = lax.axis_index("col") // 2
    rank = pivot_ref.shape[0]
    part = own_refs[0].shape[2] // 2
    for (code, own_ref, t), (_, other_ref, u) in zip(
        entries(own_refs, chips), entries(other_refs, chips)
    ):
        mine, theirs = own_ref[t], other_ref[u]
        for tile in range(2):
            where = slice(tile * part, (tile + 1) * part)
            left = jnp.where(core == 0, mine[:, where], theirs[:, where])
            right = jnp.where(core == 0, theirs[:, where], mine[:, where])
            factors_ref[chip ^ code, tile] = jnp.concatenate([left, right], axis=1)
    xrow = lanes(factors_ref, core, 0, rank)
    yrow = lanes(factors_ref, core, rank, 2 * rank)
    pbasis = jnp.concatenate(
        [lanes(factors_ref, tile, 2 * rank, 2 * rank + rank // 2) for tile in range(2)], axis=0
    )
    pcore = dot_nt(yrow, pivot_ref[...])
    lifted = dot_nn(pcore, pbasis)
    sketched = lanes(sketch_ref, 0, rank)
    corr_ref[...] = dot_nn(dot_nt(sketched, lifted), xrow)
    local = jnp.concatenate(
        [factors_ref[chip, tile, 2 * rank : 2 * rank + rank // 2, :] for tile in range(2)], axis=0
    )
    lifted = dot_nn(pcore, local)
    updated_ref[...] = panel_ref[...] - dot_nn(lifted.T, xrow)


def gram_kernel(left_ref, right_ref, corr_ref, updated_ref, range_ref, gram_ref, proj_ref):
    ranges = (left_ref[...] + right_ref[...]) - corr_ref[...]
    range_ref[...] = ranges
    proj_ref[0] = dot_nt(ranges, updated_ref[...])
    gram_ref[...] = dot_nt(ranges, ranges) / ranges.shape[1]


def factor_kernel(gram_ref, range_ref, out_ref):
    rank = gram_ref.shape[0]
    group = 8
    wide = (group, 2 * rank)
    row = lax.broadcasted_iota(jnp.int32, (group, rank), 0)
    col = lax.broadcasted_iota(jnp.int32, (group, rank), 1)
    work = [
        jnp.concatenate(
            [gram_ref[base : base + group], (row + base == col).astype(F32)], axis=1
        )
        for base in range(0, rank, group)
    ]
    rows = lax.broadcasted_iota(jnp.int32, wide, 0)

    def spread(x, lane):
        return jnp.broadcast_to(x[:, lane : lane + 1], wide)

    def pair(top, low, first, cross, second):
        det = first * second - cross * cross
        scale = 1.0 / det
        over = lambda x, y: ((x * second - y * cross) * scale, (y * first - x * cross) * scale)
        root = lax.rsqrt(first)
        done = (top * root, (low - top * (cross / first)) * (lax.rsqrt(det) * (first * root)))
        return over, done

    final = []
    for step in range(0, rank, 4):
        at, inner = divmod(step, group)
        one, two, three, four = [
            jnp.broadcast_to(work[at][inner + n : inner + n + 1], wide) for n in range(4)
        ]
        p11, p12, p13, p14 = [spread(one, step + n) for n in range(4)]
        p22, p23, p24 = [spread(two, step + n) for n in range(1, 4)]
        p33, p34, p44 = spread(three, step + 2), spread(three, step + 3), spread(four, step + 3)
        over, done = pair(one, two, p11, p12, p22)
        u1, u2 = over(one, two)
        u13, u23 = over(p13, p23)
        u14, u24 = over(p14, p24)
        three = three - (p13 * u1 + p23 * u2)
        four = four - (p14 * u1 + p24 * u2)
        over, more = pair(
            three,
            four,
            p33 - (p13 * u13 + p23 * u23),
            p34 - (p13 * u14 + p23 * u24),
            p44 - (p14 * u14 + p24 * u24),
        )
        u3, u4 = over(three, four)
        for index in range(at if inner == 0 else at + 1, len(work)):
            held = work[index]
            h1, h2, h3, h4 = [spread(held, step + n) for n in range(4)]
            h3 = h3 - (h1 * u13 + h2 * u23)
            h4 = h4 - (h1 * u14 + h2 * u24)
            work[index] = held - ((h1 * u1 + h2 * u2) + (h3 * u3 + h4 * u4))
        for n, value in enumerate(done + more):
            if inner + n == 0:
                final.append(value)
            else:
                final[at] = jnp.where(rows >= inner + n, value, final[at])
    inverse = jnp.concatenate([block[:, rank:] for block in final], axis=0)
    size = range_ref.shape[1]
    out_ref[:, :size] = dot_nn(inverse, range_ref[...])
    out_ref[:, size : size + rank] = inverse


def coeff_kernel(chips, own_ref, other_ref, perm_ref, coef_ref, *refs):
    count = (len(refs) - 3) // 2
    own_refs, other_refs = refs[:count], refs[count : 2 * count]
    basis_ref, coeff_ref, stack_ref = refs[2 * count :]
    core = lax.axis_index("col") % 2
    chip = lax.axis_index("col") // 2
    rank = own_ref.shape[0]
    size = perm_ref.shape[1]
    projected = []
    for source, pieces in ((own_ref, own_refs), (other_ref, other_refs)):
        for code, ref, t in entries(pieces, chips):
            stack_ref[chip ^ code] = ref[t]
        projected.append(dot_nn(source[:, size : size + rank], lanes(stack_ref, 0, rank)))
    both = jnp.concatenate(projected, axis=0)
    permuted = onehot_dot(both, selector_of(perm_ref[...]), ((1,), (0,)))
    result = pair_scale(permuted, coef_ref[0:1, :], coef_ref[1:2, :]) / jnp.sqrt(jnp.float32(size))
    basis_ref[core] = own_ref[:, :size]
    basis_ref[1 - core] = other_ref[:, :size]
    coeff_ref[core] = result[:rank]
    coeff_ref[1 - core] = result[rank:]


def dot3(left, right, dims):
    high, low = left.astype(BF16), None
    low = (left - high.astype(F32)).astype(BF16)
    top = right.astype(BF16)
    rest = (right - top.astype(F32)).astype(BF16)
    dot = lambda a, b: lax.dot_general(a, b, (dims, ((), ())), preferred_element_type=F32)
    return dot(high, top) + (dot(low, top) + dot(high, rest))


def left_kernel(nrow, factors_ref, *refs):
    col_refs, (left_ref, right_ref, cols_ref) = refs[:-3], refs[-3:]
    row = lax.axis_index("row")
    tiles, ncols, _, deep = left_ref.shape
    rank = deep // 3
    for code, ref, t in entries(col_refs, nrow):
        cols_ref[row ^ code] = ref[t]
    for col in range(ncols):
        basis = lanes(cols_ref, 2 * col * rank, (2 * col + 1) * rank)
        high = basis.astype(BF16)
        right_ref[col, :rank, :] = high
        right_ref[col, rank : 2 * rank, :] = high
        right_ref[col, 2 * rank :, :] = (basis - high.astype(F32)).astype(BF16)
    scaled = jnp.concatenate(
        [lanes(cols_ref, (2 * col + 1) * rank, (2 * col + 2) * rank) for col in range(ncols)],
        axis=0,
    )
    yrows = jnp.concatenate(
        [lanes(factors_ref, tile, rank, 2 * rank) for tile in range(tiles)], axis=0
    )
    core = dot3(scaled, yrows, ((1,), (1,)))
    for tile in range(tiles):
        left = dot3(
            core[:, tile * rank : (tile + 1) * rank],
            lanes(factors_ref, tile, 0, rank),
            ((1,), (0,)),
        ).T
        high = left.astype(BF16)
        low = (left - high.astype(F32)).astype(BF16)
        for col in range(ncols):
            part = slice(col * rank, (col + 1) * rank)
            left_ref[tile, col, :, :rank] = high[:, part]
            left_ref[tile, col, :, rank : 2 * rank] = low[:, part]
            left_ref[tile, col, :, 2 * rank :] = high[:, part]


def trail_kernel(trail_ref, left_ref, right_ref, out_ref):
    tile = pl.program_id(0)
    ncols, _, width = right_ref.shape
    size = left_ref.shape[2]
    groups = width // 128
    for col in range(ncols):
        change = jnp.dot(left_ref[tile, col], right_ref[col], preferred_element_type=F32)
        for group in range(groups):
            where = pl.ds(col * groups + group, size, stride=ncols * groups)
            out_ref[0, where, :] = (
                trail_ref[0, where, :] - change[:, group * 128 : (group + 1) * 128]
            )


def left_call(nrow, tiles, size, factors, cols):
    rank = factors.shape[2] * 2 // 5
    ncols = cols[0].shape[1] // (2 * rank)
    return call(
        lambda *refs: left_kernel(nrow, *refs),
        [
            jax.ShapeDtypeStruct((tiles, ncols, size, 3 * rank), BF16),
            jax.ShapeDtypeStruct((ncols, 3 * rank, nrow * cols[0].shape[2]), BF16),
        ],
        factors,
        *cols,
        scratch=[pltpu.VMEM((nrow, *cols[0].shape[1:]), F32)],
        flops=1 << 26,
    )


def trail_call(trail, left, right):
    tiles, _, size, ncols, _, width = trail.shape
    groups = width // 128
    view = trail.reshape(tiles, size * ncols * groups, 128)
    block = pl.BlockSpec((1, size * ncols * groups, 128), lambda a: (a, 0, 0))
    vmem = pl.BlockSpec(memory_space=pltpu.VMEM)
    out = pl.pallas_call(
        trail_kernel,
        out_shape=jax.ShapeDtypeStruct(view.shape, F32),
        grid=(tiles,),
        in_specs=[block, vmem, vmem],
        out_specs=block,
        cost_estimate=pl.CostEstimate(
            flops=2 * tiles * ncols * size * left.shape[3] * width,
            transcendentals=0,
            bytes_accessed=2 * view.size * 4,
        ),
        compiler_params=pltpu.CompilerParams(vmem_limit_bytes=20 << 20),
        name="trail",
    )(view, left, right)
    return out.reshape(trail.shape)


def body_of(nrow, ncol):
    chips = ncol // 2
    assert chips & (chips - 1) == 0 and nrow & (nrow - 1) == 0

    def to_core(x):
        return lax.ppermute(x, "col", [(i, i ^ 1) for i in range(ncol)])

    def to_chip(x, bit):
        return lax.ppermute(x, "col", [(i, i ^ (2 * bit)) for i in range(ncol)])

    def to_row(x, bit):
        return lax.ppermute(x, "row", [(i, i ^ bit) for i in range(nrow)])

    def body(
        trail,
        panel,
        row_basis,
        row_coeff,
        col_basis,
        col_scaled,
        pivot_basis,
        pivot_scaled,
        sketch,
        perm,
        pair_kind,
        pivot_values,
    ):
        _, _, size, part = panel.shape
        rank = sketch.shape[0]
        half = rank // 2
        width = 2 * part
        panel_t = jnp.transpose(panel[:, 0], (0, 2, 1))
        perm_row = perm.reshape(1, -1)
        panel_other = to_core(panel_t)
        inputs = (sketch, perm_row, pair_kind.reshape(1, -1), pivot_values, pivot_scaled)
        factors, columns, panel_own, *loaded, pivot_loaded = call(
            load_kernel,
            [
                shape(1, 2 * rank + half, width),
                shape(1, 2 * rank * col_basis.shape[0], col_basis.shape[3]),
                shape(part, size),
                *[jax.ShapeDtypeStruct(x.shape, x.dtype) for x in inputs],
            ],
            row_basis[:, 0],
            row_coeff[:, 0],
            pivot_basis,
            col_basis[:, 0],
            col_scaled[:, 0],
            panel_t,
            *inputs,
            kept=6 + len(inputs),
            scratch=[
                *[
                    pltpu.VMEM((x.shape[0], *x.shape[2:]), F32)
                    for x in (row_basis, row_coeff)
                ],
                pltpu.VMEM(pivot_basis.shape, F32),
                *[
                    pltpu.VMEM((x.shape[0], *x.shape[2:]), F32)
                    for x in (col_basis, col_scaled)
                ],
                pltpu.SemaphoreType.DMA((6 + len(inputs),)),
            ],
        )
        sketch_t, coef = call(
            sketch_kernel, [shape(chips, rank, width), shape(2, size)], *loaded, flops=1 << 28
        )
        total, panel_mine = call(
            partial_kernel,
            [shape(rank, size), shape(width, size)],
            sketch_t,
            panel_own,
            panel_other,
            flops=1 << 26,
        )
        own = gather(factors, chips, to_chip)
        cols = gather(columns, nrow, to_row)
        bits = stages(chips)[::-1]
        for bit in bits[:-1]:
            remote = to_chip(total, bit)
            total = call(add_kernel, shape(rank, size), total, remote)
        remote = to_chip(total, bits[-1])
        other = []
        for piece in own:
            other.append(to_core(piece))
        factors_all, corr, updated = call(
            lambda *refs: prepare_kernel(chips, *refs),
            [shape(chips, 2, 2 * rank + half, width), shape(rank, size), shape(width, size)],
            pivot_loaded,
            *own,
            *other,
            sketch_t,
            panel_mine,
            flops=1 << 26,
        )
        ranges, gram, proj = call(
            gram_kernel,
            [shape(rank, size), shape(rank, rank), shape(1, rank, width)],
            total,
            remote,
            corr,
            updated,
            flops=1 << 26,
        )
        projs = gather(proj, chips, to_chip)
        basis = call(factor_kernel, shape(rank, size + 128), gram, ranges, flops=1 << 28)
        basis_other = to_core(basis)
        left, right = left_call(nrow, 2, size, factors_all, cols)
        trail_out = trail_call(trail, left, right)
        projs_other = []
        for piece in projs:
            projs_other.append(to_core(piece))
        basis_out, coeff_out = call(
            lambda *refs: coeff_kernel(chips, *refs),
            [shape(2, rank, size)] * 2,
            basis,
            basis_other,
            loaded[1],
            coef,
            *projs,
            *projs_other,
            scratch=[pltpu.VMEM((chips, rank, width), F32)],
            flops=1 << 28,
        )
        return (trail_out, basis_out[:, None], coeff_out[:, None])

    return body


def solution(mesh):
    step = body_of(mesh.shape["row"], mesh.shape["col"])

    return jax.shard_map(
        step,
        mesh=mesh,
        in_specs=(
            P(None, "row", None, None, "col", None),
            P(None, "row", None, "col"),
            P(None, "row", None, "col"),
            P(None, "row", None, "col"),
            P(None, "col", None, "row"),
            P(None, "col", None, "row"),
            P(None, "col"),
            P(),
            P(),
            P(),
            P(),
            P(),
        ),
        out_specs=(
            P(None, "row", None, None, "col", None),
            P(None, "row", None, None),
            P(None, "row", None, None),
        ),
        check_vma=False,
    )
```

profile of v0, /device:TPU:0, one launch (start us, length us, event | category | flops | bytes accessed | tf_op | source)
XLA Modules:
  0.0 45.1 jit_solution(16220692239121735092)
XLA Ops:
  0.6 0.0 copy-start
  0.6 0.6 %collective-permute-start.4 = (f32[2,64,512]{2,1,0:T(8,128)}, f32[2,64,512]{2,1,0:T(8,128)S(1)}, u32[]{:S(2)}, u32[]{:S(2)}) collective-permute-start(f32[2,64,512]{2,1,0:T(8,128)} %bitcast.19), channel_id=1, source_target_pairs={{0,1},{1,0},{2,3},{3,2},{4,5},{5,4},{6,7},{7,6},{8,9},{9,8},{10,11... | collective-permute-start | bytes 786440 | tf_op jit(solution)/shard_map/ppermute | solution.py:460
  1.2 1.6 %shard_map.139 = (f32[1,160,128]{2,1,0:T(8,128)S(1)}, f32[1,256,128]{2,1,0:T(8,128)S(1)}, f32[64,512]{1,0:T(8,128)S(1)}, f32[64,512]{1,0:T(8,128)S(1)}, s32[1,51...) custom-call(f32[2,64,64]{2,1,0:T(8,128)} %bitcast.21, ...), custom_call_target="tpu_custom_call" | custom-call | bytes 1048576 | tf_op jit(solution)/shard_map/pallas_call | solution.py:73
  2.8 3.5 %collective-permute-start = (f32[1,160,128]{2,1,0:T(8,128)S(1)}, f32[1,160,128]{2,1,0:T(8,128)S(1)}, u32[]{:S(2)}, u32[]{:S(2)}) collective-permute-start(f32[1,160,128]{2,1,0:T(8,128)S(1)} %get-tuple-element.26.refs_0_), channel_id=1, source_target_pairs={{0,4},{1,5},{2,6},{3,7},{4,0},{5,1},{6,2},{7,3},{8,12},{9,13},{10,... | collective-permute-start | bytes 245768 | tf_op jit(solution)/shard_map/ppermute | solution.py:463
  6.3 5.0 %collective-permute-done.refs_1_ = f32[1,160,128]{2,1,0:T(8,128)S(1)} collective-permute-done((f32[1,160,128]{2,1,0:T(8,128)S(1)}, f32[1,160,128]{2,1,0:T(8,128)S(1)}, u32[]{:S(2)}, u32[]{:S(2)}) %collective-permute-start) | collective-permute-done | bytes 81952 | tf_op jit(solution)/shard_map/ppermute | solution.py:463
  11.4 0.8 %collective-permute-start.1 = (f32[2,160,128]{2,1,0:T(8,128)S(1)}, f32[2,160,128]{2,1,0:T(8,128)S(1)}, u32[]{:S(2)}, u32[]{:S(2)}) collective-permute-start(f32[2,160,128]{2,1,0:T(8,128)S(1)} %shard_map.140.refs_1_), channel_id=1, source_target_pairs={{0,2},{1,3},{2,0},{3,1},{4,6},{5,7},{6,4},{7,5},{8,10},{9,11},{10,... | collective-permute-start | bytes 491528 | tf_op jit(solution)/shard_map/ppermute | solution.py:463
  12.2 0.5 %shard_map.141 = (f32[4,64,128]{2,1,0:T(8,128)S(1)}, f32[2,512]{1,0:T(2,128)S(1)}) custom-call(f32[64,512]{1,0:T(8,128)S(1)} %get-tuple-element.27.refs_0_, s32[1,512]{1,0:T(1,128)S(1)} %get-tuple-element.28.refs_1_.refs_2_, s32[1,256]{1,0:T(1,128)S(1)} %get-tuple-element.29.refs_2_, f32[3,256]{1,0:T(4,128)S(1)} %get-tuple-element.30.refs_3_), custom_call_target="tpu_custom_call" | custom-call | flops 268435456 | bytes 1048576 | tf_op jit(solution)/shard_map/pallas_call | solution.py:73
  12.7 0.0 collective-permute-done.4.refs_2_
  12.7 0.3 shard_map.142
  13.0 1.3 %collective-permute-start.7 = (f32[64,512]{1,0:T(8,128)S(1)}, f32[64,512]{1,0:T(8,128)S(1)}, u32[]{:S(2)}, u32[]{:S(2)}) collective-permute-start(f32[64,512]{1,0:T(8,128)S(1)} %get-tuple-element.38.refs_0_), channel_id=1, source_target_pairs={{0,2},{1,3},{2,0},{3,1},{4,6},{5,7},{6,4},{7,5},{8,10},{9,11},{10,... | collective-permute-start | bytes 393224 | tf_op jit(solution)/shard_map/ppermute | solution.py:463
  14.3 1.6 %collective-permute-start.5 = (f32[1,256,128]{2,1,0:T(8,128)S(1)}, f32[1,256,128]{2,1,0:T(8,128)S(1)}, u32[]{:S(2)}, u32[]{:S(2)}) collective-permute-start(f32[1,256,128]{2,1,0:T(8,128)S(1)} %get-tuple-element.35.refs_0_), channel_id=1, source_target_pairs={{0,16},{8,24},{16,0},{24,8},{1,17},{9,25},{17,1},{25,9},{2,18},{10... | collective-permute-start | bytes 393224 | tf_op jit(solution)/shard_map/ppermute | solution.py:466
  15.9 0.0 collective-permute-start.2
  15.9 2.5 %collective-permute-done.1.refs_2_ = f32[2,160,128]{2,1,0:T(8,128)S(1)} collective-permute-done((f32[2,160,128]{2,1,0:T(8,128)S(1)}, f32[2,160,128]{2,1,0:T(8,128)S(1)}, u32[]{:S(2)}, u32[]{:S(2)}) %collective-permute-start.1) | collective-permute-done | bytes 163872 | tf_op jit(solution)/shard_map/ppermute | solution.py:463
  18.5 0.0 collective-permute-start.3
  18.5 2.0 %collective-permute-done.7.refs_1_ = f32[64,512]{1,0:T(8,128)S(1)} collective-permute-done((f32[64,512]{1,0:T(8,128)S(1)}, f32[64,512]{1,0:T(8,128)S(1)}, u32[]{:S(2)}, u32[]{:S(2)}) %collective-permute-start.7) | collective-permute-done | bytes 131104 | tf_op jit(solution)/shard_map/ppermute | solution.py:463
  20.5 2.4 %collective-permute-start.8 = (f32[64,512]{1,0:T(8,128)S(1)}, f32[64,512]{1,0:T(8,128)S(1)}, u32[]{:S(2)}, u32[]{:S(2)}) collective-permute-start(f32[64,512]{1,0:T(8,128)S(1)} %shard_map.146.refs_0_), channel_id=1, source_target_pairs={{0,4},{1,5},{2,6},{3,7},{4,0},{5,1},{6,2},{7,3},{8,12},{9,13},{10,... | collective-permute-start | bytes 393224 | tf_op jit(solution)/shard_map/ppermute | solution.py:463
  22.9 0.0 collective-permute-done.5.refs_1_
  22.9 1.6 %collective-permute-start.6 = (f32[2,256,128]{2,1,0:T(8,128)S(1)}, f32[2,256,128]{2,1,0:T(8,128)S(1)}, u32[]{:S(2)}, u32[]{:S(2)}) collective-permute-start(f32[2,256,128]{2,1,0:T(8,128)S(1)} %shard_map.144.refs_1_), channel_id=1, source_target_pairs={{0,8},{8,0},{16,24},{24,16},{1,9},{9,1},{17,25},{25,17},{2,10},{10... | collective-permute-start | bytes 786440 | tf_op jit(solution)/shard_map/ppermute | solution.py:466
  24.5 0.0 collective-permute-done.2.refs_3_
  24.5 0.0 collective-permute-done.3.refs_4_
  24.5 1.6 %shard_map.143 = (f32[4,2,160,128]{3,2,1,0:T(8,128)S(1)}, f32[64,512]{1,0:T(8,128)S(1)}, f32[128,512]{1,0:T(8,128)S(1)}) custom-call(f32[64,512]{1,0:T(8,128)S(1)} %get-tuple-element.25.refs_0_, f32[2,160,128]{2,1,0:T(8,128)S(1)} %shard_map.140.refs_1_, f32[2,160,128]{2,1,0:T(8,128)S(1)} %collective-permute-done.1.refs_2_, ...), custom_call_target="tpu_custom_call" | custom-call | flops 67108864 | bytes 1048576 | tf_op jit(solution)/shard_map/pallas_call | solution.py:73
  26.1 2.8 %collective-permute-done.8.refs_1_ = f32[64,512]{1,0:T(8,128)S(1)} collective-permute-done((f32[64,512]{1,0:T(8,128)S(1)}, f32[64,512]{1,0:T(8,128)S(1)}, u32[]{:S(2)}, u32[]{:S(2)}) %collective-permute-start.8) | collective-permute-done | bytes 131104 | tf_op jit(solution)/shard_map/ppermute | solution.py:463
  28.9 0.5 %shard_map.147 = (f32[64,512]{1,0:T(8,128)S(1)}, f32[64,64]{1,0:T(8,128)S(1)}, f32[1,64,128]{2,1,0:T(8,128)S(1)}) custom-call(f32[64,512]{1,0:T(8,128)S(1)} %shard_map.146.refs_0_, f32[64,512]{1,0:T(8,128)S(1)} %collective-permute-done.8.refs_1_, f32[64,512]{1,0:T(8,128)S(1)} %get-tuple-element.39.refs_2_, f32[128,512]{1,0:T(8,128)S(1)} %get-tuple-element.40.refs_3_), custom_call_target="tpu_custom_call" | custom-call | flops 67108864 | bytes 1048576 | tf_op jit(solution)/shard_map/pallas_call | solution.py:73
  29.4 0.1 collective-permute-start.10
  29.5 2.9 %shard_map.148.refs_0_ = f32[64,640]{1,0:T(8,128)S(1)} custom-call(f32[64,64]{1,0:T(8,128)S(1)} %get-tuple-element.41.refs_0_, f32[64,512]{1,0:T(8,128)S(1)} %get-tuple-element.42.refs_1_), custom_call_target="tpu_custom_call" | custom-call | flops 268435456 | bytes 1048576 | tf_op jit(solution)/shard_map/pallas_call | solution.py:73
  32.4 0.1 collective-permute-start.9
  32.5 2.4 %collective-permute-done.10.refs_1_ = f32[1,64,128]{2,1,0:T(8,128)S(1)} collective-permute-done((f32[1,64,128]{2,1,0:T(8,128)S(1)}, f32[1,64,128]{2,1,0:T(8,128)S(1)}, u32[]{:S(2)}, u32[]{:S(2)}) %collective-permute-start.10) | collective-permute-done | bytes 32800 | tf_op jit(solution)/shard_map/ppermute | solution.py:463
  34.9 1.8 %collective-permute-start.11 = (f32[2,64,128]{2,1,0:T(8,128)S(1)}, f32[2,64,128]{2,1,0:T(8,128)S(1)}, u32[]{:S(2)}, u32[]{:S(2)}) collective-permute-start(f32[2,64,128]{2,1,0:T(8,128)S(1)} %shard_map.149.refs_4_), channel_id=1, source_target_pairs={{0,2},{1,3},{2,0},{3,1},{4,6},{5,7},{6,4},{7,5},{8,10},{9,11},{10,... | collective-permute-start | bytes 196616 | tf_op jit(solution)/shard_map/ppermute | solution.py:463
  36.7 0.2 collective-permute-start.12
  36.9 2.5 %collective-permute-done.11.refs_5_ = f32[2,64,128]{2,1,0:T(8,128)S(1)} collective-permute-done((f32[2,64,128]{2,1,0:T(8,128)S(1)}, f32[2,64,128]{2,1,0:T(8,128)S(1)}, u32[]{:S(2)}, u32[]{:S(2)}) %collective-permute-start.11) | collective-permute-done | bytes 65568 | tf_op jit(solution)/shard_map/ppermute | solution.py:463
  39.4 0.0 collective-permute-start.13
  39.4 0.0 collective-permute-done.6.refs_2_
  39.4 1.2 %shard_map.145 = (bf16[2,2,512,192]{3,2,1,0:T(8,128)(2,1)S(1)}, bf16[2,192,512]{2,1,0:T(8,128)(2,1)S(1)}) custom-call(f32[4,2,160,128]{3,2,1,0:T(8,128)S(1)} %get-tuple-element.34.refs_0_, f32[2,256,128]{2,1,0:T(8,128)S(1)} %shard_map.144.refs_1_, f32[2,256,128]{2,1,0:T(8,128)S(1)} %collective-permute-done.6.refs_2_), custom_call_target="tpu_custom_call" | custom-call | flops 67108864 | bytes 1048576 | tf_op jit(solution)/shard_map/pallas_call | solution.py:73
  40.6 0.0 copy-done
  40.6 2.9 %trail.1 = f32[2,4096,128]{2,1,0:T(8,128)} custom-call(f32[2,4096,128]{2,1,0:T(8,128)S(1)} %bitcast.17, bf16[2,2,512,192]{3,2,1,0:T(8,128)(2,1)S(1)} %get-tuple-element.36.left_ref, bf16[2,192,512]{2,1,0:T(8,128)(2,1)S(1)} %get-tuple-element.37.right_ref), custom_call_target="tpu_custom_call" | custom-call | flops 402653184 | bytes 8388608 | tf_op jit(solution)/shard_map/trail/pallas_call | solution.py:438
  43.5 0.0 collective-permute-done.12.refs_6_
  43.5 0.0 collective-permute-done.13.refs_7_
  43.5 0.0 collective-permute-done.9.refs_1_
  43.5 1.6 %shard_map.150 = (f32[2,64,512]{2,1,0:T(8,128)}, f32[2,64,512]{2,1,0:T(8,128)}) custom-call(f32[64,640]{1,0:T(8,128)S(1)} %shard_map.148.refs_0_, f32[64,640]{1,0:T(8,128)S(1)} %collective-permute-done.9.refs_1_, s32[1,512]{1,0:T(1,128)S(1)} %get-tuple-element.28.refs_1_.refs_2_, f32[2,512]{1,0:T(2,128)S(1)} %get-tuple-element.43.refs_3_, ...), custom_call_target="tpu_custom_call" | custom-call | flops 268435456 | bytes 1048576 | tf_op jit(solution)/shard_map/pallas_call | solution.py:73
  (4 shorter events, 0.0 us)
Async XLA Ops:
  0.6 40.0 %copy-start = (f32[2,1,512,2,1,512]{5,4,3,2,1,0:T(1,128)S(1)}, f32[2,1,512,2,1,512]{5,4,3,2,1,0:T(1,128)}, u32[]{:S(2)}) copy-start(f32[2,1,512,2,1,512]{5,4,3,2,1,0:T(1,128)} %param.12) | copy-start | bytes 12582916
  0.6 12.1 %collective-permute-start.4 = (f32[2,64,512]{2,1,0:T(8,128)}, f32[2,64,512]{2,1,0:T(8,128)S(1)}, u32[]{:S(2)}, u32[]{:S(2)}) collective-permute-start(f32[2,64,512]{2,1,0:T(8,128)} %bitcast.19), channel_id=1, source_target_pairs={{0,1},{1,0},{2,3},{3,2},{4,5},{5,4},{6,7},{7,6},{8,9},{9,8},{10,11... | collective-permute-start | bytes 786440 | tf_op jit(solution)/shard_map/ppermute | solution.py:460
  2.8 8.6 %collective-permute-start = (f32[1,160,128]{2,1,0:T(8,128)S(1)}, f32[1,160,128]{2,1,0:T(8,128)S(1)}, u32[]{:S(2)}, u32[]{:S(2)}) collective-permute-start(f32[1,160,128]{2,1,0:T(8,128)S(1)} %get-tuple-element.26.refs_0_), channel_id=1, source_target_pairs={{0,4},{1,5},{2,6},{3,7},{4,0},{5,1},{6,2},{7,3},{8,12},{9,13},{10,... | collective-permute-start | bytes 245768 | tf_op jit(solution)/shard_map/ppermute | solution.py:463
  11.4 7.1 %collective-permute-start.1 = (f32[2,160,128]{2,1,0:T(8,128)S(1)}, f32[2,160,128]{2,1,0:T(8,128)S(1)}, u32[]{:S(2)}, u32[]{:S(2)}) collective-permute-start(f32[2,160,128]{2,1,0:T(8,128)S(1)} %shard_map.140.refs_1_), channel_id=1, source_target_pairs={{0,2},{1,3},{2,0},{3,1},{4,6},{5,7},{6,4},{7,5},{8,10},{9,11},{10,... | collective-permute-start | bytes 491528 | tf_op jit(solution)/shard_map/ppermute | solution.py:463
  13.0 7.4 %collective-permute-start.7 = (f32[64,512]{1,0:T(8,128)S(1)}, f32[64,512]{1,0:T(8,128)S(1)}, u32[]{:S(2)}, u32[]{:S(2)}) collective-permute-start(f32[64,512]{1,0:T(8,128)S(1)} %get-tuple-element.38.refs_0_), channel_id=1, source_target_pairs={{0,2},{1,3},{2,0},{3,1},{4,6},{5,7},{6,4},{7,5},{8,10},{9,11},{10,... | collective-permute-start | bytes 393224 | tf_op jit(solution)/shard_map/ppermute | solution.py:463
  14.3 8.6 %collective-permute-start.5 = (f32[1,256,128]{2,1,0:T(8,128)S(1)}, f32[1,256,128]{2,1,0:T(8,128)S(1)}, u32[]{:S(2)}, u32[]{:S(2)}) collective-permute-start(f32[1,256,128]{2,1,0:T(8,128)S(1)} %get-tuple-element.35.refs_0_), channel_id=1, source_target_pairs={{0,16},{8,24},{16,0},{24,8},{1,17},{9,25},{17,1},{25,9},{2,18},{10... | collective-permute-start | bytes 393224 | tf_op jit(solution)/shard_map/ppermute | solution.py:466
  15.9 8.6 %collective-permute-start.2 = (f32[2,160,128]{2,1,0:T(8,128)S(1)}, f32[2,160,128]{2,1,0:T(8,128)S(1)}, u32[]{:S(2)}, u32[]{:S(2)}) collective-permute-start(f32[2,160,128]{2,1,0:T(8,128)S(1)} %shard_map.140.refs_1_), channel_id=1, source_target_pairs={{0,1},{1,0},{2,3},{3,2},{4,5},{5,4},{6,7},{7,6},{8,9},{9,8},{10,11... | collective-permute-start | bytes 491528 | tf_op jit(solution)/shard_map/ppermute | solution.py:460
  18.5 6.0 %collective-permute-start.3 = (f32[2,160,128]{2,1,0:T(8,128)S(1)}, f32[2,160,128]{2,1,0:T(8,128)S(1)}, u32[]{:S(2)}, u32[]{:S(2)}) collective-permute-start(f32[2,160,128]{2,1,0:T(8,128)S(1)} %collective-permute-done.1.refs_2_), channel_id=1, source_target_pairs={{0,1},{1,0},{2,3},{3,2},{4,5},{5,4},{6,7},{7,6},{8,9},{9,8},{10,11... | collective-permute-start | bytes 491528 | tf_op jit(solution)/shard_map/ppermute | solution.py:460
  20.5 8.4 %collective-permute-start.8 = (f32[64,512]{1,0:T(8,128)S(1)}, f32[64,512]{1,0:T(8,128)S(1)}, u32[]{:S(2)}, u32[]{:S(2)}) collective-permute-start(f32[64,512]{1,0:T(8,128)S(1)} %shard_map.146.refs_0_), channel_id=1, source_target_pairs={{0,4},{1,5},{2,6},{3,7},{4,0},{5,1},{6,2},{7,3},{8,12},{9,13},{10,... | collective-permute-start | bytes 393224 | tf_op jit(solution)/shard_map/ppermute | solution.py:463
  22.9 16.5 %collective-permute-start.6 = (f32[2,256,128]{2,1,0:T(8,128)S(1)}, f32[2,256,128]{2,1,0:T(8,128)S(1)}, u32[]{:S(2)}, u32[]{:S(2)}) collective-permute-start(f32[2,256,128]{2,1,0:T(8,128)S(1)} %shard_map.144.refs_1_), channel_id=1, source_target_pairs={{0,8},{8,0},{16,24},{24,16},{1,9},{9,1},{17,25},{25,17},{2,10},{10... | collective-permute-start | bytes 786440 | tf_op jit(solution)/shard_map/ppermute | solution.py:466
  29.4 5.5 %collective-permute-start.10 = (f32[1,64,128]{2,1,0:T(8,128)S(1)}, f32[1,64,128]{2,1,0:T(8,128)S(1)}, u32[]{:S(2)}, u32[]{:S(2)}) collective-permute-start(f32[1,64,128]{2,1,0:T(8,128)S(1)} %get-tuple-element.44.refs_0_), channel_id=1, source_target_pairs={{0,4},{1,5},{2,6},{3,7},{4,0},{5,1},{6,2},{7,3},{8,12},{9,13},{10,... | collective-permute-start | bytes 98312 | tf_op jit(solution)/shard_map/ppermute | solution.py:463
  32.4 11.1 %collective-permute-start.9 = (f32[64,640]{1,0:T(8,128)S(1)}, f32[64,640]{1,0:T(8,128)S(1)}, u32[]{:S(2)}, u32[]{:S(2)}) collective-permute-start(f32[64,640]{1,0:T(8,128)S(1)} %shard_map.148.refs_0_), channel_id=1, source_target_pairs={{0,1},{1,0},{2,3},{3,2},{4,5},{5,4},{6,7},{7,6},{8,9},{9,8},{10,11... | collective-permute-start | bytes 491528 | tf_op jit(solution)/shard_map/ppermute | solution.py:460
  34.9 4.5 %collective-permute-start.11 = (f32[2,64,128]{2,1,0:T(8,128)S(1)}, f32[2,64,128]{2,1,0:T(8,128)S(1)}, u32[]{:S(2)}, u32[]{:S(2)}) collective-permute-start(f32[2,64,128]{2,1,0:T(8,128)S(1)} %shard_map.149.refs_4_), channel_id=1, source_target_pairs={{0,2},{1,3},{2,0},{3,1},{4,6},{5,7},{6,4},{7,5},{8,10},{9,11},{10,... | collective-permute-start | bytes 196616 | tf_op jit(solution)/shard_map/ppermute | solution.py:463
  36.7 6.8 %collective-permute-start.12 = (f32[2,64,128]{2,1,0:T(8,128)S(1)}, f32[2,64,128]{2,1,0:T(8,128)S(1)}, u32[]{:S(2)}, u32[]{:S(2)}) collective-permute-start(f32[2,64,128]{2,1,0:T(8,128)S(1)} %shard_map.149.refs_4_), channel_id=1, source_target_pairs={{0,1},{1,0},{2,3},{3,2},{4,5},{5,4},{6,7},{7,6},{8,9},{9,8},{10,11... | collective-permute-start | bytes 196616 | tf_op jit(solution)/shard_map/ppermute | solution.py:460
  39.4 4.1 %collective-permute-start.13 = (f32[2,64,128]{2,1,0:T(8,128)S(1)}, f32[2,64,128]{2,1,0:T(8,128)S(1)}, u32[]{:S(2)}, u32[]{:S(2)}) collective-permute-start(f32[2,64,128]{2,1,0:T(8,128)S(1)} %collective-permute-done.11.refs_5_), channel_id=1, source_target_pairs={{0,1},{1,0},{2,3},{3,2},{4,5},{5,4},{6,7},{7,6},{8,9},{9,8},{10,11... | collective-permute-start | bytes 196616 | tf_op jit(solution)/shard_map/ppermute | solution.py:460
where the time goes:
time: 45.3 us; the launch traced here: 45.1 us
  waiting for transfers between devices  17.3 us (38%)
  starting transfers between devices  14 us (31%)
  Pallas kernels  13.1 us (29%)
  between operations  0.76 us (2%)
    ppermute x6, waiting for transfers between devices, to_chip(): return lax.ppermute(x, 'col', [(i, i ^ 2 * bit) for i in range(ncol)])  17.3 us
    pallas_call x12, Pallas kernels, call(): pl.pallas_call(wrapped, out_shape=outs, in_specs=[hbm] * (fetched + kept)...  10.3 us
    ppermute x6, starting transfers between devices, to_chip(): return lax.ppermute(x, 'col', [(i, i ^ 2 * bit) for i in range(ncol)])  9.95 us
    ppermute x2, starting transfers between devices, to_row(): return lax.ppermute(x, 'row', [(i, i ^ bit) for i in range(nrow)])  3.16 us
    pallas_call x1, Pallas kernels, trail_call(): pl.pallas_call(trail_kernel, out_shape=jax.ShapeDtypeStruct(view.shape, F...  2.85 us
  transfers between devices with their start and end apart: 14, of which 6 were waited for; matrix products, arithmetic and copies ran while one was open for 0% of the time, Pallas kernels for 26%

commit v1 on v0

--- a/solution.py
+++ b/solution.py
@@ -42,7 +42,7 @@
     return parts[:rows] + (parts[rows : 2 * rows] + parts[2 * rows :])
 
 
-def call(kernel, outs, *args, fetched=0, kept=0, scratch=(), flops=0):
+def call(kernel, outs, *args, fetched=0, kept=0, placed=0, scratch=(), flops=0):
     vmem = pl.BlockSpec(memory_space=pltpu.VMEM)
     hbm = pl.BlockSpec(memory_space=pltpu.HBM)
     many = isinstance(outs, (list, tuple))
@@ -74,7 +74,7 @@
         wrapped,
         out_shape=outs,
         in_specs=[hbm] * (fetched + kept) + [vmem] * (len(args) - fetched - kept),
-        out_specs=[vmem] * len(outs) if many else vmem,
+        out_specs=[hbm] * placed + [vmem] * (len(outs) - placed) if many else vmem,
         scratch_shapes=scratch,
         cost_estimate=pl.CostEstimate(flops=flops, transcendentals=0, bytes_accessed=1 << 20),
         compiler_params=pltpu.CompilerParams(vmem_limit_bytes=8 << 20),
@@ -99,7 +99,9 @@
     return (row == perm).astype(F32).astype(BF16)
 
 
-def sketch_kernel(sketch_ref, perm_ref, kind_ref, values_ref, out_ref, coef_ref):
+def sketch_kernel(
+    sketch_ref, perm_ref, kind_ref, values_ref, out_ref, coef_ref, selector_ref
+):
     pairs = kind_ref.shape[1]
     length = perm_ref.shape[1]
     one, two, cross = values_ref[0:1, :], values_ref[1:2, :], values_ref[2:3, :]
@@ -121,7 +123,9 @@
     coef_ref[0:1, :] = diag
     coef_ref[1:2, :] = off
     scaled = pair_scale(sketch_ref[...], diag, off)
-    placed = onehot_dot(scaled, selector_of(perm_ref[...]), ((1,), (1,)))
+    selector = selector_of(perm_ref[...])
+    selector_ref[...] = selector
+    placed = onehot_dot(scaled, selector, ((1,), (1,)))
     chips, _, width = out_ref.shape
     for chip in range(chips):
         out_ref[chip] = placed[:, chip * width : (chip + 1) * width]
@@ -136,9 +140,9 @@
     return bits
 
 
-def codes(size):
-    order = [0]
-    for bit in stages(size):
+def codes(bits, start=(0,)):
+    order = list(start)
+    for bit in bits:
         order = order + [code ^ bit for code in order]
     return order
 
@@ -156,16 +160,15 @@
     return call(stack_kernel, shape(total, *pieces[0].shape[1:]), *pieces)
 
 
-def gather(x, size, send):
+def gather(x, bits, send):
     pieces = [x]
-    for bit in stages(size):
+    for bit in bits:
         held = pieces[0] if len(pieces) == 1 else stack(*pieces)
         pieces = [held, send(held, bit)]
     return pieces
 
 
-def entries(refs, size):
-    order = codes(size)
+def entries(refs, order):
     at = 0
     for ref in refs:
         for t in range(ref.shape[0]):
@@ -187,8 +190,8 @@
     targets, buffers, sems = refs[7 + count : 7 + 2 * count], refs[7 + 2 * count : -1], refs[-1]
     core = lax.axis_index("col") % 2
     pairs = list(zip(packed, buffers))
-    for source, target in zip(sources, targets):
-        pairs.append((source.at[core] if len(source.shape) == 3 else source, target))
+    for n, (source, target) in enumerate(zip(sources, targets)):
+        pairs.append((source.at[core] if n == 0 else source, target))
     copies = [
         pltpu.make_async_copy(source, target, sems.at[n])
         for n, (source, target) in enumerate(pairs)
@@ -214,29 +217,34 @@
         copy.wait()
 
 
-def partial_kernel(sketch_ref, own_ref, other_ref, out_ref, panel_ref):
+def join_kernel(own_ref, other_ref, out_ref):
     core = lax.axis_index("col") % 2
+    part = own_ref.shape[0]
+    out_ref[pl.ds(pl.multiple_of(core * part, part), part), :] = own_ref[...]
+    out_ref[pl.ds(pl.multiple_of((1 - core) * part, part), part), :] = other_ref[core]
+
+
+def partial_kernel(sketch_ref, own_ref, near_ref, out_ref):
     chip = lax.axis_index("col") // 2
-    part = own_ref.shape[0]
-    panel_ref[pl.ds(pl.multiple_of(core * part, part), part), :] = own_ref[...]
-    panel_ref[pl.ds(pl.multiple_of((1 - core) * part, part), part), :] = other_ref[core]
-    out_ref[...] = dot_nn(sketch_ref[chip], panel_ref[...])
+    out_ref[...] = dot_nn(sketch_ref[chip], own_ref[...]) + dot_nn(
+        sketch_ref[chip ^ 1], near_ref[...]
+    )
 
 
 def add_kernel(left_ref, right_ref, out_ref):
     out_ref[...] = left_ref[...] + right_ref[...]
 
 
-def prepare_kernel(chips, pivot_ref, *refs):
-    count = (len(refs) - 5) // 2
+def prepare_kernel(order, pivot_ref, *refs):
+    count = (len(refs) - 6) // 2
     own_refs, other_refs = refs[:count], refs[count : 2 * count]
-    sketch_ref, panel_ref, factors_ref, corr_ref, updated_ref = refs[2 * count :]
+    sketch_ref, *panel_refs, factors_ref, corr_ref, updated_ref = refs[2 * count :]
     core = lax.axis_index("col") % 2
     chip = lax.axis_index("col") // 2
     rank = pivot_ref.shape[0]
     part = own_refs[0].shape[2] // 2
     for (code, own_ref, t), (_, other_ref, u) in zip(
-        entries(own_refs, chips), entries(other_refs, chips)
+        entries(own_refs, order), entries(other_refs, order)
     ):
         mine, theirs = own_ref[t], other_ref[u]
         for tile in range(2):
@@ -250,21 +258,40 @@
         [lanes(factors_ref, tile, 2 * rank, 2 * rank + rank // 2) for tile in range(2)], axis=0
     )
     pcore = dot_nt(yrow, pivot_ref[...])
-    lifted = dot_nn(pcore, pbasis)
-    sketched = lanes(sketch_ref, 0, rank)
-    corr_ref[...] = dot_nn(dot_nt(sketched, lifted), xrow)
+    mixed = dot_nt(dot_nt(lanes(sketch_ref, 0, rank), pbasis), pcore)
     local = jnp.concatenate(
-        [factors_ref[chip, tile, 2 * rank : 2 * rank + rank // 2, :] for tile in range(2)], axis=0
-    )
-    lifted = dot_nn(pcore, local)
-    updated_ref[...] = panel_ref[...] - dot_nn(lifted.T, xrow)
+        [
+            jnp.concatenate(
+                [
+                    factors_ref[chip ^ slot, tile, 2 * rank : 2 * rank + rank // 2, :]
+                    for tile in range(2)
+                ],
+                axis=0,
+            )
+            for slot in range(len(panel_refs))
+        ],
+        axis=1,
+    )
+    sides = jnp.concatenate([mixed, dot_nn(pcore, local).T], axis=0)
+    change = dot_nn(sides, xrow)
+    corr_ref[...] = change[:rank]
+    at = rank
+    for slot, panel_ref in enumerate(panel_refs):
+        deep = panel_ref.shape[0]
+        updated_ref[slot] = panel_ref[...] - change[at : at + deep]
+        at += deep
 
 
 def gram_kernel(left_ref, right_ref, corr_ref, updated_ref, range_ref, gram_ref, proj_ref):
     ranges = (left_ref[...] + right_ref[...]) - corr_ref[...]
     range_ref[...] = ranges
-    proj_ref[0] = dot_nt(ranges, updated_ref[...])
-    gram_ref[...] = dot_nt(ranges, ranges) / ranges.shape[1]
+    slots, width, size = updated_ref.shape
+    products = dot_nt(
+        ranges, jnp.concatenate([updated_ref[slot] for slot in range(slots)] + [ranges], axis=0)
+    )
+    for slot in range(slots):
+        proj_ref[slot] = products[:, slot * width : (slot + 1) * width]
+    gram_ref[...] = products[:, slots * width :] / size
 
 
 def factor_kernel(gram_ref, range_ref, out_ref):
@@ -332,26 +359,37 @@
     out_ref[:, size : size + rank] = inverse
 
 
-def coeff_kernel(chips, own_ref, other_ref, perm_ref, coef_ref, *refs):
-    count = (len(refs) - 3) // 2
-    own_refs, other_refs = refs[:count], refs[count : 2 * count]
-    basis_ref, coeff_ref, stack_ref = refs[2 * count :]
+def coeff_of(order, basis_ref, selector_ref, coef_ref, piece_refs, stack_ref):
+    chip = lax.axis_index("col") // 2
+    rank = basis_ref.shape[0]
+    size = selector_ref.shape[1]
+    for code, ref, t in entries(piece_refs, order):
+        stack_ref[chip ^ code] = ref[t]
+    projected = dot_nn(basis_ref[:, size : size + rank], lanes(stack_ref, 0, rank))
+    permuted = onehot_dot(projected, selector_ref[...], ((1,), (0,)))
+    return pair_scale(permuted, coef_ref[0:1, :], coef_ref[1:2, :]) / jnp.sqrt(jnp.float32(size))
+
+
+def coeff_kernel(order, basis_ref, other_ref, selector_ref, coef_ref, *refs):
     core = lax.axis_index("col") % 2
-    chip = lax.axis_index("col") // 2
-    rank = own_ref.shape[0]
-    size = perm_ref.shape[1]
-    projected = []
-    for source, pieces in ((own_ref, own_refs), (other_ref, other_refs)):
-        for code, ref, t in entries(pieces, chips):
-            stack_ref[chip ^ code] = ref[t]
-        projected.append(dot_nn(source[:, size : size + rank], lanes(stack_ref, 0, rank)))
-    both = jnp.concatenate(projected, axis=0)
-    permuted = onehot_dot(both, selector_of(perm_ref[...]), ((1,), (0,)))
-    result = pair_scale(permuted, coef_ref[0:1, :], coef_ref[1:2, :]) / jnp.sqrt(jnp.float32(size))
-    basis_ref[core] = own_ref[:, :size]
-    basis_ref[1 - core] = other_ref[:, :size]
-    coeff_ref[core] = result[:rank]
-    coeff_ref[1 - core] = result[rank:]
+    basis_out_ref, out_ref, stack_ref, sems = refs[-4:]
+    size = selector_ref.shape[1]
+    copies = [
+        pltpu.make_async_copy(source.at[:, :size], basis_out_ref.at[tile], sems.at[n])
+        for n, (source, tile) in enumerate(((basis_ref, core), (other_ref, 1 - core)))
+    ]
+    for copy in copies:
+        copy.start()
+    out_ref[...] = coeff_of(order, basis_ref, selector_ref, coef_ref, refs[:-4], stack_ref)
+    for copy in copies:
+        copy.wait()
+
+
+def finish_kernel(order, basis_ref, selector_ref, coef_ref, own_ref, *refs):
+    core = lax.axis_index("col") % 2
+    out_ref, stack_ref = refs[-2:]
+    out_ref[core] = own_ref[...]
+    out_ref[1 - core] = coeff_of(order, basis_ref, selector_ref, coef_ref, refs[:-2], stack_ref)
 
 
 def dot3(left, right, dims):
@@ -363,12 +401,12 @@
     return dot(high, top) + (dot(low, top) + dot(high, rest))
 
 
-def left_kernel(nrow, factors_ref, *refs):
+def left_kernel(order, factors_ref, *refs):
     col_refs, (left_ref, right_ref, cols_ref) = refs[:-3], refs[-3:]
     row = lax.axis_index("row")
     tiles, ncols, _, deep = left_ref.shape
     rank = deep // 3
-    for code, ref, t in entries(col_refs, nrow):
+    for code, ref, t in entries(col_refs, order):
         cols_ref[row ^ code] = ref[t]
     for col in range(ncols):
         basis = lanes(cols_ref, 2 * col * rank, (2 * col + 1) * rank)
@@ -399,25 +437,45 @@
             left_ref[tile, col, :, 2 * rank :] = high[:, part]
 
 
-def trail_kernel(trail_ref, left_ref, right_ref, out_ref):
-    tile = pl.program_id(0)
-    ncols, _, width = right_ref.shape
-    size = left_ref.shape[2]
-    groups = width // 128
-    for col in range(ncols):
-        change = jnp.dot(left_ref[tile, col], right_ref[col], preferred_element_type=F32)
-        for group in range(groups):
-            where = pl.ds(col * groups + group, size, stride=ncols * groups)
-            out_ref[0, where, :] = (
-                trail_ref[0, where, :] - change[:, group * 128 : (group + 1) * 128]
+def trail_kernel(trail_ref, left_ref, right_ref, out_ref, change_ref, held_ref, sems):
+    tiles, ncols, size, _ = left_ref.shape
+    groups = right_ref.shape[2] // 128
+    step = ncols * groups
+    chunks = sems.shape[1]
+    rows = size // chunks
+    copies = []
+    for tile in range(tiles):
+        for col in range(ncols):
+            change_ref[col] = jnp.dot(
+                left_ref[tile, col], right_ref[col], preferred_element_type=F32
             )
-
-
-def left_call(nrow, tiles, size, factors, cols):
+        for chunk in range(chunks):
+            for col in range(ncols):
+                for group in range(groups):
+                    where = pl.ds(chunk * rows * step + col * groups + group, rows, stride=step)
+                    held_ref[tile, where, :] = (
+                        trail_ref[tile, where, :]
+                        - change_ref[
+                            col,
+                            chunk * rows : (chunk + 1) * rows,
+                            group * 128 : (group + 1) * 128,
+                        ]
+                    )
+            part = pl.ds(chunk * rows * step, rows * step)
+            copy = pltpu.make_async_copy(
+                held_ref.at[tile, part], out_ref.at[tile, part], sems.at[tile, chunk]
+            )
+            copy.start()
+            copies.append(copy)
+    for copy in copies:
+        copy.wait()
+
+
+def left_call(nrow, order, tiles, size, factors, cols):
     rank = factors.shape[2] * 2 // 5
     ncols = cols[0].shape[1] // (2 * rank)
     return call(
-        lambda *refs: left_kernel(nrow, *refs),
+        lambda *refs: left_kernel(order, *refs),
         [
             jax.ShapeDtypeStruct((tiles, ncols, size, 3 * rank), BF16),
             jax.ShapeDtypeStruct((ncols, 3 * rank, nrow * cols[0].shape[2]), BF16),
@@ -429,18 +487,21 @@
     )
 
 
-def trail_call(trail, left, right):
+def trail_call(trail, left, right, chunks=4):
     tiles, _, size, ncols, _, width = trail.shape
-    groups = width // 128
-    view = trail.reshape(tiles, size * ncols * groups, 128)
-    block = pl.BlockSpec((1, size * ncols * groups, 128), lambda a: (a, 0, 0))
+    rows = size * ncols * width // 128
+    view = trail.reshape(tiles, rows, 128)
     vmem = pl.BlockSpec(memory_space=pltpu.VMEM)
     out = pl.pallas_call(
         trail_kernel,
         out_shape=jax.ShapeDtypeStruct(view.shape, F32),
-        grid=(tiles,),
-        in_specs=[block, vmem, vmem],
-        out_specs=block,
+        in_specs=[vmem] * 3,
+        out_specs=pl.BlockSpec(memory_space=pltpu.HBM),
+        scratch_shapes=[
+            pltpu.VMEM((ncols, size, width), F32),
+            pltpu.VMEM(view.shape, F32),
+            pltpu.SemaphoreType.DMA((tiles, chunks)),
+        ],
         cost_estimate=pl.CostEstimate(
             flops=2 * tiles * ncols * size * left.shape[3] * width,
             transcendentals=0,
@@ -454,7 +515,7 @@
 
 def body_of(nrow, ncol):
     chips = ncol // 2
-    assert chips & (chips - 1) == 0 and nrow & (nrow - 1) == 0
+    assert chips > 2 and chips & (chips - 1) == 0 and nrow & (nrow - 1) == 0
 
     def to_core(x):
         return lax.ppermute(x, "col", [(i, i ^ 1) for i in range(ncol)])
@@ -485,8 +546,12 @@
         width = 2 * part
         panel_t = jnp.transpose(panel[:, 0], (0, 2, 1))
         perm_row = perm.reshape(1, -1)
+        bits = stages(chips)
+        order = codes(bits)
+        pair_order = codes(bits[:-1], (0, 1))
         panel_other = to_core(panel_t)
         inputs = (sketch, perm_row, pair_kind.reshape(1, -1), pivot_values, pivot_scaled)
+        packed = (row_basis[:, 0], row_coeff[:, 0], pivot_basis, col_basis[:, 0], col_scaled[:, 0])
         factors, columns, panel_own, *loaded, pivot_loaded = call(
             load_kernel,
             [
@@ -495,85 +560,88 @@
                 shape(part, size),
                 *[jax.ShapeDtypeStruct(x.shape, x.dtype) for x in inputs],
             ],
-            row_basis[:, 0],
-            row_coeff[:, 0],
-            pivot_basis,
-            col_basis[:, 0],
-            col_scaled[:, 0],
+            *packed,
             panel_t,
             *inputs,
             kept=6 + len(inputs),
             scratch=[
-                *[
-                    pltpu.VMEM((x.shape[0], *x.shape[2:]), F32)
-                    for x in (row_basis, row_coeff)
-                ],
-                pltpu.VMEM(pivot_basis.shape, F32),
-                *[
-                    pltpu.VMEM((x.shape[0], *x.shape[2:]), F32)
-                    for x in (col_basis, col_scaled)
-                ],
+                *[pltpu.VMEM(x.shape, F32) for x in packed],
                 pltpu.SemaphoreType.DMA((6 + len(inputs),)),
             ],
         )
-        sketch_t, coef = call(
-            sketch_kernel, [shape(chips, rank, width), shape(2, size)], *loaded, flops=1 << 28
-        )
-        total, panel_mine = call(
-            partial_kernel,
-            [shape(rank, size), shape(width, size)],
-            sketch_t,
-            panel_own,
-            panel_other,
-            flops=1 << 26,
-        )
-        own = gather(factors, chips, to_chip)
-        cols = gather(columns, nrow, to_row)
-        bits = stages(chips)[::-1]
-        for bit in bits[:-1]:
+        panel_mine = call(join_kernel, shape(width, size), panel_own, panel_other)
+        near = to_chip(panel_mine, 1)
+        own = gather(factors, bits, to_chip)
+        cols = gather(columns, stages(nrow), to_row)
+        sketch_t, coef, selector = call(
+            sketch_kernel,
+            [shape(chips, rank, width), shape(2, size), jax.ShapeDtypeStruct((size, size), BF16)],
+            *loaded,
+            flops=1 << 28,
+        )
+        total = call(partial_kernel, shape(rank, size), sketch_t, panel_mine, near, flops=1 << 26)
+        sums = bits[:-1][::-1]
+        for bit in sums[:-1]:
             remote = to_chip(total, bit)
             total = call(add_kernel, shape(rank, size), total, remote)
-        remote = to_chip(total, bits[-1])
+        remote = to_chip(total, sums[-1])
         other = []
         for piece in own:
             other.append(to_core(piece))
         factors_all, corr, updated = call(
-            lambda *refs: prepare_kernel(chips, *refs),
-            [shape(chips, 2, 2 * rank + half, width), shape(rank, size), shape(width, size)],
+            lambda *refs: prepare_kernel(order, *refs),
+            [
+                shape(chips, 2, 2 * rank + half, width),
+                shape(rank, size),
+                shape(2, width, size),
+            ],
             pivot_loaded,
             *own,
             *other,
             sketch_t,
             panel_mine,
+            near,
             flops=1 << 26,
         )
         ranges, gram, proj = call(
             gram_kernel,
-            [shape(rank, size), shape(rank, rank), shape(1, rank, width)],
+            [shape(rank, size), shape(rank, rank), shape(2, rank, width)],
             total,
             remote,
             corr,
             updated,
             flops=1 << 26,
         )
-        projs = gather(proj, chips, to_chip)
+        projs = gather(proj, bits[:-1], to_chip)
         basis = call(factor_kernel, shape(rank, size + 128), gram, ranges, flops=1 << 28)
         basis_other = to_core(basis)
-        left, right = left_call(nrow, 2, size, factors_all, cols)
+        left, right = left_call(nrow, codes(stages(nrow)), 2, size, factors_all, cols)
         trail_out = trail_call(trail, left, right)
         projs_other = []
         for piece in projs:
             projs_other.append(to_core(piece))
-        basis_out, coeff_out = call(
-            lambda *refs: coeff_kernel(chips, *refs),
-            [shape(2, rank, size)] * 2,
+        scratch = [pltpu.VMEM((chips, rank, width), F32)]
+        basis_out, coeff = call(
+            lambda *refs: coeff_kernel(pair_order, *refs),
+            [shape(2, rank, size), shape(rank, size)],
             basis,
             basis_other,
-            loaded[1],
+            selector,
             coef,
             *projs,
+            placed=1,
+            scratch=[*scratch, pltpu.SemaphoreType.DMA((2,))],
+            flops=1 << 28,
+        )
+        coeff_out = call(
+            lambda *refs: finish_kernel(pair_order, *refs),
+            shape(2, rank, size),
+            basis_other,
+            selector,
+            coef,
+            coeff,
             *projs_other,
-            scratch=[pltpu.VMEM((chips, rank, width), F32)],
+            scratch=scratch,
             flops=1 << 28,
         )
         return (trail_out, basis_out[:, None], coeff_out[:, None])

time: 45.3 us -> 46.5 us (1.026)
  waiting for transfers between devices: 17.3 us -> 19.7 us
  starting transfers between devices: 14 us -> 11.7 us
  Pallas kernels: 13.1 us -> 14.1 us
    ppermute x6 -> x5, starting transfers between devices: 9.95 us -> 7.48 us  [to_chip(): return lax.ppermute(x, 'col', [(i, i ^ 2 * bit) for i in range(ncol)])]
    ppermute x6 -> x5, waiting for transfers between devices: 17.3 us -> 19.7 us  [to_chip(): return lax.ppermute(x, 'col', [(i, i ^ 2 * bit) for i in range(ncol)])]
    pallas_call x12, Pallas kernels: 10.3 us -> 11.4 us  [call(): pl.pallas_call(wrapped, out_shape=outs, in_specs=[hbm] * (fetched + kept)...]
  transfers between devices with their start and end apart: 14 -> 13, of which waited for: 6 -> 4; matrix products, arithmetic and copies ran while one was open for 0% -> 0% of each run, Pallas kernels for 26% -> 28%
where the time goes in v1:
time: 46.5 us; the launch traced here: 46.3 us
  waiting for transfers between devices  19.7 us (42%)
  Pallas kernels  14.1 us (30%)
  starting transfers between devices  11.7 us (25%)
  between operations  0.79 us (2%)
    ppermute x5, waiting for transfers between devices, to_chip(): return lax.ppermute(x, 'col', [(i, i ^ 2 * bit) for i in range(ncol)])  19.7 us
    pallas_call x12, Pallas kernels, call(): pl.pallas_call(wrapped, out_shape=outs, in_specs=[hbm] * (fetched + kept)...  11.4 us
    ppermute x5, starting transfers between devices, to_chip(): return lax.ppermute(x, 'col', [(i, i ^ 2 * bit) for i in range(ncol)])  7.48 us
    ppermute x2, starting transfers between devices, to_row(): return lax.ppermute(x, 'row', [(i, i ^ bit) for i in range(nrow)])  3.07 us
    pallas_call x1, Pallas kernels, trail_call(): pl.pallas_call(trail_kernel, out_shape=jax.ShapeDtypeStruct(view.shape, F...  2.75 us
    ppermute x6, starting transfers between devices, to_core(): return lax.ppermute(x, 'col', [(i, i ^ 1) for i in range(ncol)])  1.12 us
  transfers between devices with their start and end apart: 13, of which 4 were waited for; matrix products, arithmetic and copies ran while one was open for 0% of the time, Pallas kernels for 28%

profile of v1, /device:TPU:0, one launch (start us, length us, event | category | flops | bytes accessed | tf_op | source)
XLA Modules:
  0.0 46.3 jit_solution(3558270574755362194)
XLA Ops:
  0.6 0.6 %collective-permute-start.4 = (f32[2,64,512]{2,1,0:T(8,128)}, f32[2,64,512]{2,1,0:T(8,128)S(1)}, u32[]{:S(2)}, u32[]{:S(2)}) collective-permute-start(f32[2,64,512]{2,1,0:T(8,128)} %bitcast.20), channel_id=1, source_target_pairs={{0,1},{1,0},{2,3},{3,2},{4,5},{5,4},{6,7},{7,6},{8,9},{9,8},{10,11... | collective-permute-start | bytes 786440 | tf_op jit(solution)/shard_map/ppermute | solution.py:521
  1.2 0.0 copy-start
  1.2 1.4 %shard_map.139 = (f32[1,160,128]{2,1,0:T(8,128)S(1)}, f32[1,256,128]{2,1,0:T(8,128)S(1)}, f32[64,512]{1,0:T(8,128)S(1)}, f32[64,512]{1,0:T(8,128)S(1)}, s32[1,51...) custom-call(f32[2,64,64]{2,1,0:T(8,128)} %bitcast.22, ...), custom_call_target="tpu_custom_call" | custom-call | bytes 1048576 | tf_op jit(solution)/shard_map/pallas_call | solution.py:73
  2.6 3.7 %collective-permute-start = (f32[1,160,128]{2,1,0:T(8,128)S(1)}, f32[1,160,128]{2,1,0:T(8,128)S(1)}, u32[]{:S(2)}, u32[]{:S(2)}) collective-permute-start(f32[1,160,128]{2,1,0:T(8,128)S(1)} %get-tuple-element.25.refs_0_), channel_id=1, source_target_pairs={{0,4},{1,5},{2,6},{3,7},{4,0},{5,1},{6,2},{7,3},{8,12},{9,13},{10,... | collective-permute-start | bytes 245768 | tf_op jit(solution)/shard_map/ppermute | solution.py:524
  6.3 0.0 collective-permute-done.4.refs_1_
  6.3 1.6 %collective-permute-start.5 = (f32[128,512]{1,0:T(8,128)S(1)}, f32[128,512]{1,0:T(8,128)S(1)}, u32[]{:S(2)}, u32[]{:S(2)}) collective-permute-start(f32[128,512]{1,0:T(8,128)S(1)} %shard_map.142.refs_6_.refs_1_), channel_id=1, source_target_pairs={{0,2},{1,3},{2,0},{3,1},{4,6},{5,7},{6,4},{7,5},{8,10},{9,11},{10,... | collective-permute-start | bytes 786440 | tf_op jit(solution)/shard_map/ppermute | solution.py:524
  8.0 3.3 %collective-permute-done.refs_1_ = f32[1,160,128]{2,1,0:T(8,128)S(1)} collective-permute-done((f32[1,160,128]{2,1,0:T(8,128)S(1)}, f32[1,160,128]{2,1,0:T(8,128)S(1)}, u32[]{:S(2)}, u32[]{:S(2)}) %collective-permute-start) | collective-permute-done | bytes 81952 | tf_op jit(solution)/shard_map/ppermute | solution.py:524
  11.3 0.8 %collective-permute-start.1 = (f32[2,160,128]{2,1,0:T(8,128)S(1)}, f32[2,160,128]{2,1,0:T(8,128)S(1)}, u32[]{:S(2)}, u32[]{:S(2)}) collective-permute-start(f32[2,160,128]{2,1,0:T(8,128)S(1)} %shard_map.140.refs_1_), channel_id=1, source_target_pairs={{0,2},{1,3},{2,0},{3,1},{4,6},{5,7},{6,4},{7,5},{8,10},{9,11},{10,... | collective-permute-start | bytes 491528 | tf_op jit(solution)/shard_map/ppermute | solution.py:524
  12.0 1.5 %collective-permute-start.6 = (f32[1,256,128]{2,1,0:T(8,128)S(1)}, f32[1,256,128]{2,1,0:T(8,128)S(1)}, u32[]{:S(2)}, u32[]{:S(2)}) collective-permute-start(f32[1,256,128]{2,1,0:T(8,128)S(1)} %get-tuple-element.33.refs_0_), channel_id=1, source_target_pairs={{0,16},{8,24},{16,0},{24,8},{1,17},{9,25},{17,1},{25,9},{2,18},{10... | collective-permute-start | bytes 393224 | tf_op jit(solution)/shard_map/ppermute | solution.py:527
  13.5 0.0 collective-permute-start.2
  13.5 5.4 %collective-permute-done.1.refs_2_ = f32[2,160,128]{2,1,0:T(8,128)S(1)} collective-permute-done((f32[2,160,128]{2,1,0:T(8,128)S(1)}, f32[2,160,128]{2,1,0:T(8,128)S(1)}, u32[]{:S(2)}, u32[]{:S(2)}) %collective-permute-start.1) | collective-permute-done | bytes 163872 | tf_op jit(solution)/shard_map/ppermute | solution.py:524
  18.9 0.0 collective-permute-start.3
  18.9 0.6 %shard_map.141 = (f32[4,64,128]{2,1,0:T(8,128)S(1)}, f32[2,512]{1,0:T(2,128)S(1)}, bf16[512,512]{1,0:T(8,128)(2,1)S(1)}) custom-call(f32[64,512]{1,0:T(8,128)S(1)} %get-tuple-element.26.refs_0_, s32[1,512]{1,0:T(1,128)S(1)} %get-tuple-element.27.refs_1_, s32[1,256]{1,0:T(1,128)S(1)} %get-tuple-element.28.refs_2_, f32[3,256]{1,0:T(4,128)S(1)} %get-tuple-element.29.refs_3_), custom_call_target="tpu_custom_call" | custom-call | flops 268435456 | bytes 1048576 | tf_op jit(solution)/shard_map/pallas_call | solution.py:73
  19.5 0.0 collective-permute-done.5.refs_7_.refs_2_
  19.5 0.4 shard_map.146.refs_0_
  19.9 1.3 %collective-permute-start.8 = (f32[64,512]{1,0:T(8,128)S(1)}, f32[64,512]{1,0:T(8,128)S(1)}, u32[]{:S(2)}, u32[]{:S(2)}) collective-permute-start(f32[64,512]{1,0:T(8,128)S(1)} %shard_map.146.refs_0_), channel_id=1, source_target_pairs={{0,4},{1,5},{2,6},{3,7},{4,0},{5,1},{6,2},{7,3},{8,12},{9,13},{10,... | collective-permute-start | bytes 393224 | tf_op jit(solution)/shard_map/ppermute | solution.py:524
  21.2 0.0 collective-permute-done.6.refs_1_
  21.3 1.6 %collective-permute-start.7 = (f32[2,256,128]{2,1,0:T(8,128)S(1)}, f32[2,256,128]{2,1,0:T(8,128)S(1)}, u32[]{:S(2)}, u32[]{:S(2)}) collective-permute-start(f32[2,256,128]{2,1,0:T(8,128)S(1)} %shard_map.144.refs_1_), channel_id=1, source_target_pairs={{0,8},{8,0},{16,24},{24,16},{1,9},{9,1},{17,25},{25,17},{2,10},{10... | collective-permute-start | bytes 786440 | tf_op jit(solution)/shard_map/ppermute | solution.py:527
  22.8 0.0 collective-permute-done.2.refs_3_
  22.8 0.0 collective-permute-done.3.refs_4_
  22.8 1.5 %shard_map.143 = (f32[4,2,160,128]{3,2,1,0:T(8,128)S(1)}, f32[64,512]{1,0:T(8,128)S(1)}, f32[2,128,512]{2,1,0:T(8,128)S(1)}) custom-call(f32[64,512]{1,0:T(8,128)S(1)} %get-tuple-element.24.refs_0_, f32[2,160,128]{2,1,0:T(8,128)S(1)} %shard_map.140.refs_1_, f32[2,160,128]{2,1,0:T(8,128)S(1)} %collective-permute-done.1.refs_2_, ...), custom_call_target="tpu_custom_call" | custom-call | flops 67108864 | bytes 1048576 | tf_op jit(solution)/shard_map/pallas_call | solution.py:73
  24.3 5.2 %collective-permute-done.8.refs_1_ = f32[64,512]{1,0:T(8,128)S(1)} collective-permute-done((f32[64,512]{1,0:T(8,128)S(1)}, f32[64,512]{1,0:T(8,128)S(1)}, u32[]{:S(2)}, u32[]{:S(2)}) %collective-permute-start.8) | collective-permute-done | bytes 131104 | tf_op jit(solution)/shard_map/ppermute | solution.py:524
  29.6 0.7 %shard_map.147 = (f32[64,512]{1,0:T(8,128)S(1)}, f32[64,64]{1,0:T(8,128)S(1)}, f32[2,64,128]{2,1,0:T(8,128)S(1)}) custom-call(f32[64,512]{1,0:T(8,128)S(1)} %shard_map.146.refs_0_, f32[64,512]{1,0:T(8,128)S(1)} %collective-permute-done.8.refs_1_, f32[64,512]{1,0:T(8,128)S(1)} %get-tuple-element.36.refs_2_, f32[2,128,512]{2,1,0:T(8,128)S(1)} %get-tuple-element.37.refs_3_), custom_call_target="tpu_custom_call" | custom-call | flops 67108864 | bytes 1048576 | tf_op jit(solution)/shard_map/pallas_call | solution.py:73
  30.3 2.9 %shard_map.148.refs_0_ = f32[64,640]{1,0:T(8,128)S(1)} custom-call(f32[64,64]{1,0:T(8,128)S(1)} %get-tuple-element.38.refs_0_, f32[64,512]{1,0:T(8,128)S(1)} %get-tuple-element.39.refs_1_), custom_call_target="tpu_custom_call" | custom-call | flops 268435456 | bytes 1048576 | tf_op jit(solution)/shard_map/pallas_call | solution.py:73
  33.3 0.1 collective-permute-start.9
  33.4 0.1 collective-permute-start.10
  33.4 0.4 collective-permute-start.11
  33.9 5.8 %collective-permute-done.10.refs_5_ = f32[2,64,128]{2,1,0:T(8,128)S(1)} collective-permute-done((f32[2,64,128]{2,1,0:T(8,128)S(1)}, f32[2,64,128]{2,1,0:T(8,128)S(1)}, u32[]{:S(2)}, u32[]{:S(2)}) %collective-permute-start.10) | collective-permute-done | bytes 65568 | tf_op jit(solution)/shard_map/ppermute | solution.py:524
  39.7 0.1 collective-permute-start.12
  39.7 0.0 collective-permute-done.7.refs_2_
  39.7 1.2 %shard_map.145 = (bf16[2,2,512,192]{3,2,1,0:T(8,128)(2,1)S(1)}, bf16[2,192,512]{2,1,0:T(8,128)(2,1)S(1)}) custom-call(f32[4,2,160,128]{3,2,1,0:T(8,128)S(1)} %get-tuple-element.32.refs_0_, f32[2,256,128]{2,1,0:T(8,128)S(1)} %shard_map.144.refs_1_, f32[2,256,128]{2,1,0:T(8,128)S(1)} %collective-permute-done.7.refs_2_), custom_call_target="tpu_custom_call" | custom-call | flops 67108864 | bytes 1048576 | tf_op jit(solution)/shard_map/pallas_call | solution.py:73
  40.9 0.0 copy-done
  41.0 2.8 %trail.1 = f32[2,4096,128]{2,1,0:T(8,128)} custom-call(f32[2,4096,128]{2,1,0:T(8,128)S(1)} %bitcast.17, bf16[2,2,512,192]{3,2,1,0:T(8,128)(2,1)S(1)} %get-tuple-element.34.left_ref, bf16[2,192,512]{2,1,0:T(8,128)(2,1)S(1)} %get-tuple-element.35.right_ref), custom_call_target="tpu_custom_call" | custom-call | flops 402653184 | bytes 8388608 | tf_op jit(solution)/shard_map/trail/pallas_call | solution.py:495
  43.7 0.0 collective-permute-done.9.refs_1_.refs_0_
  43.7 1.2 %shard_map.149 = (f32[2,64,512]{2,1,0:T(8,128)}, f32[64,512]{1,0:T(8,128)S(1)}) custom-call(f32[64,640]{1,0:T(8,128)S(1)} %shard_map.148.refs_0_, f32[64,640]{1,0:T(8,128)S(1)} %collective-permute-done.9.refs_1_.refs_0_, bf16[512,512]{1,0:T(8,128)(2,1)S(1)} %get-tuple-element.40.refs_2_.refs_1_, f32[2,512]{1,0:T(2,128)S(1)} %get-tuple-element.41.refs_3_.refs_2_, ...), custom_call_target="tpu_custom_call" | custom-call | flops 268435456 | bytes 1048576 | tf_op jit(solution)/shard_map/pallas_call | solution.py:73
  45.0 0.0 collective-permute-done.11.refs_4_
  45.0 0.0 collective-permute-done.12.refs_5_
  45.0 1.3 %shard_map.150 = f32[2,64,512]{2,1,0:T(8,128)} custom-call(f32[64,640]{1,0:T(8,128)S(1)} %collective-permute-done.9.refs_1_.refs_0_, bf16[512,512]{1,0:T(8,128)(2,1)S(1)} %get-tuple-element.40.refs_2_.refs_1_, f32[2,512]{1,0:T(2,128)S(1)} %get-tuple-element.41.refs_3_.refs_2_, f32[64,512]{1,0:T(8,128)S(1)} %get-tuple-element.44.refs_3_, ...), custom_call_target="tpu_custom_call" | custom-call | flops 268435456 | bytes 1048576 | tf_op jit(solution)/shard_map/pallas_call | solution.py:73
  (3 shorter events, 0.1 us)
Async XLA Ops:
  0.6 5.7 %collective-permute-start.4 = (f32[2,64,512]{2,1,0:T(8,128)}, f32[2,64,512]{2,1,0:T(8,128)S(1)}, u32[]{:S(2)}, u32[]{:S(2)}) collective-permute-start(f32[2,64,512]{2,1,0:T(8,128)} %bitcast.20), channel_id=1, source_target_pairs={{0,1},{1,0},{2,3},{3,2},{4,5},{5,4},{6,7},{7,6},{8,9},{9,8},{10,11... | collective-permute-start | bytes 786440 | tf_op jit(solution)/shard_map/ppermute | solution.py:521
  1.2 39.8 %copy-start = (f32[2,1,512,2,1,512]{5,4,3,2,1,0:T(1,128)S(1)}, f32[2,1,512,2,1,512]{5,4,3,2,1,0:T(1,128)}, u32[]{:S(2)}) copy-start(f32[2,1,512,2,1,512]{5,4,3,2,1,0:T(1,128)} %param.12) | copy-start | bytes 12582916
  2.6 8.6 %collective-permute-start = (f32[1,160,128]{2,1,0:T(8,128)S(1)}, f32[1,160,128]{2,1,0:T(8,128)S(1)}, u32[]{:S(2)}, u32[]{:S(2)}) collective-permute-start(f32[1,160,128]{2,1,0:T(8,128)S(1)} %get-tuple-element.25.refs_0_), channel_id=1, source_target_pairs={{0,4},{1,5},{2,6},{3,7},{4,0},{5,1},{6,2},{7,3},{8,12},{9,13},{10,... | collective-permute-start | bytes 245768 | tf_op jit(solution)/shard_map/ppermute | solution.py:524
  6.3 13.2 %collective-permute-start.5 = (f32[128,512]{1,0:T(8,128)S(1)}, f32[128,512]{1,0:T(8,128)S(1)}, u32[]{:S(2)}, u32[]{:S(2)}) collective-permute-start(f32[128,512]{1,0:T(8,128)S(1)} %shard_map.142.refs_6_.refs_1_), channel_id=1, source_target_pairs={{0,2},{1,3},{2,0},{3,1},{4,6},{5,7},{6,4},{7,5},{8,10},{9,11},{10,... | collective-permute-start | bytes 786440 | tf_op jit(solution)/shard_map/ppermute | solution.py:524
  11.3 7.7 %collective-permute-start.1 = (f32[2,160,128]{2,1,0:T(8,128)S(1)}, f32[2,160,128]{2,1,0:T(8,128)S(1)}, u32[]{:S(2)}, u32[]{:S(2)}) collective-permute-start(f32[2,160,128]{2,1,0:T(8,128)S(1)} %shard_map.140.refs_1_), channel_id=1, source_target_pairs={{0,2},{1,3},{2,0},{3,1},{4,6},{5,7},{6,4},{7,5},{8,10},{9,11},{10,... | collective-permute-start | bytes 491528 | tf_op jit(solution)/shard_map/ppermute | solution.py:524
  12.0 9.2 %collective-permute-start.6 = (f32[1,256,128]{2,1,0:T(8,128)S(1)}, f32[1,256,128]{2,1,0:T(8,128)S(1)}, u32[]{:S(2)}, u32[]{:S(2)}) collective-permute-start(f32[1,256,128]{2,1,0:T(8,128)S(1)} %get-tuple-element.33.refs_0_), channel_id=1, source_target_pairs={{0,16},{8,24},{16,0},{24,8},{1,17},{9,25},{17,1},{25,9},{2,18},{10... | collective-permute-start | bytes 393224 | tf_op jit(solution)/shard_map/ppermute | solution.py:527
  13.5 9.3 %collective-permute-start.2 = (f32[2,160,128]{2,1,0:T(8,128)S(1)}, f32[2,160,128]{2,1,0:T(8,128)S(1)}, u32[]{:S(2)}, u32[]{:S(2)}) collective-permute-start(f32[2,160,128]{2,1,0:T(8,128)S(1)} %shard_map.140.refs_1_), channel_id=1, source_target_pairs={{0,1},{1,0},{2,3},{3,2},{4,5},{5,4},{6,7},{7,6},{8,9},{9,8},{10,11... | collective-permute-start | bytes 491528 | tf_op jit(solution)/shard_map/ppermute | solution.py:521
  18.9 3.9 %collective-permute-start.3 = (f32[2,160,128]{2,1,0:T(8,128)S(1)}, f32[2,160,128]{2,1,0:T(8,128)S(1)}, u32[]{:S(2)}, u32[]{:S(2)}) collective-permute-start(f32[2,160,128]{2,1,0:T(8,128)S(1)} %collective-permute-done.1.refs_2_), channel_id=1, source_target_pairs={{0,1},{1,0},{2,3},{3,2},{4,5},{5,4},{6,7},{7,6},{8,9},{9,8},{10,11... | collective-permute-start | bytes 491528 | tf_op jit(solution)/shard_map/ppermute | solution.py:521
  19.9 9.7 %collective-permute-start.8 = (f32[64,512]{1,0:T(8,128)S(1)}, f32[64,512]{1,0:T(8,128)S(1)}, u32[]{:S(2)}, u32[]{:S(2)}) collective-permute-start(f32[64,512]{1,0:T(8,128)S(1)} %shard_map.146.refs_0_), channel_id=1, source_target_pairs={{0,4},{1,5},{2,6},{3,7},{4,0},{5,1},{6,2},{7,3},{8,12},{9,13},{10,... | collective-permute-start | bytes 393224 | tf_op jit(solution)/shard_map/ppermute | solution.py:524
  21.3 18.5 %collective-permute-start.7 = (f32[2,256,128]{2,1,0:T(8,128)S(1)}, f32[2,256,128]{2,1,0:T(8,128)S(1)}, u32[]{:S(2)}, u32[]{:S(2)}) collective-permute-start(f32[2,256,128]{2,1,0:T(8,128)S(1)} %shard_map.144.refs_1_), channel_id=1, source_target_pairs={{0,8},{8,0},{16,24},{24,16},{1,9},{9,1},{17,25},{25,17},{2,10},{10... | collective-permute-start | bytes 786440 | tf_op jit(solution)/shard_map/ppermute | solution.py:527
  33.3 10.4 %collective-permute-start.9 = (f32[64,640]{1,0:T(8,128)S(1)}, f32[64,640]{1,0:T(8,128)S(1)}, u32[]{:S(2)}, u32[]{:S(2)}) collective-permute-start(f32[64,640]{1,0:T(8,128)S(1)} %shard_map.148.refs_0_), channel_id=1, source_target_pairs={{0,1},{1,0},{2,3},{3,2},{4,5},{5,4},{6,7},{7,6},{8,9},{9,8},{10,11... | collective-permute-start | bytes 491528 | tf_op jit(solution)/shard_map/ppermute | solution.py:521
  33.4 6.3 %collective-permute-start.10 = (f32[2,64,128]{2,1,0:T(8,128)S(1)}, f32[2,64,128]{2,1,0:T(8,128)S(1)}, u32[]{:S(2)}, u32[]{:S(2)}) collective-permute-start(f32[2,64,128]{2,1,0:T(8,128)S(1)} %get-tuple-element.42.refs_4_), channel_id=1, source_target_pairs={{0,4},{1,5},{2,6},{3,7},{4,0},{5,1},{6,2},{7,3},{8,12},{9,13},{10,... | collective-permute-start | bytes 196616 | tf_op jit(solution)/shard_map/ppermute | solution.py:524
  33.4 11.5 %collective-permute-start.11 = (f32[2,64,128]{2,1,0:T(8,128)S(1)}, f32[2,64,128]{2,1,0:T(8,128)S(1)}, u32[]{:S(2)}, u32[]{:S(2)}) collective-permute-start(f32[2,64,128]{2,1,0:T(8,128)S(1)} %get-tuple-element.42.refs_4_), channel_id=1, source_target_pairs={{0,1},{1,0},{2,3},{3,2},{4,5},{5,4},{6,7},{7,6},{8,9},{9,8},{10,11... | collective-permute-start | bytes 196616 | tf_op jit(solution)/shard_map/ppermute | solution.py:521
  39.7 5.3 %collective-permute-start.12 = (f32[2,64,128]{2,1,0:T(8,128)S(1)}, f32[2,64,128]{2,1,0:T(8,128)S(1)}, u32[]{:S(2)}, u32[]{:S(2)}) collective-permute-start(f32[2,64,128]{2,1,0:T(8,128)S(1)} %collective-permute-done.10.refs_5_), channel_id=1, source_target_pairs={{0,1},{1,0},{2,3},{3,2},{4,5},{5,4},{6,7},{7,6},{8,9},{9,8},{10,11... | collective-permute-start | bytes 196616 | tf_op jit(solution)/shard_map/ppermute | solution.py:521

commit v2 on v1

--- a/solution.py
+++ b/solution.py
@@ -196,7 +196,7 @@
         pltpu.make_async_copy(source, target, sems.at[n])
         for n, (source, target) in enumerate(pairs)
     ]
-    for copy in copies:
+    for copy in copies[5:6] + copies[:5] + copies[6:]:
         copy.start()
     for copy in copies[:5]:
         copy.wait()
@@ -282,27 +282,32 @@
         at += deep
 
 
-def gram_kernel(left_ref, right_ref, corr_ref, updated_ref, range_ref, gram_ref, proj_ref):
+def project_kernel(left_ref, right_ref, corr_ref, updated_ref, range_ref, proj_ref):
     ranges = (left_ref[...] + right_ref[...]) - corr_ref[...]
     range_ref[...] = ranges
-    slots, width, size = updated_ref.shape
+    slots, width, _ = updated_ref.shape
     products = dot_nt(
-        ranges, jnp.concatenate([updated_ref[slot] for slot in range(slots)] + [ranges], axis=0)
+        ranges, jnp.concatenate([updated_ref[slot] for slot in range(slots)], axis=0)
     )
     for slot in range(slots):
         proj_ref[slot] = products[:, slot * width : (slot + 1) * width]
-    gram_ref[...] = products[:, slots * width :] / size
-
-
-def factor_kernel(gram_ref, range_ref, out_ref):
-    rank = gram_ref.shape[0]
+
+
+def factor_kernel(
+    range_ref, trail_ref, left_ref, right_ref, out_ref, trail_out_ref, held_ref, sems
+):
+    trail_parts, trail_copies = trail_work(
+        trail_ref, left_ref, right_ref, trail_out_ref, held_ref, sems
+    )
+    rank = range_ref.shape[0]
+    gram = dot_nt(range_ref[...], range_ref[...]) / range_ref.shape[1]
     group = 8
     wide = (group, 2 * rank)
     row = lax.broadcasted_iota(jnp.int32, (group, rank), 0)
     col = lax.broadcasted_iota(jnp.int32, (group, rank), 1)
     work = [
         jnp.concatenate(
-            [gram_ref[base : base + group], (row + base == col).astype(F32)], axis=1
+            [gram[base : base + group], (row + base == col).astype(F32)], axis=1
         )
         for base in range(0, rank, group)
     ]
@@ -348,6 +353,9 @@
             h3 = h3 - (h1 * u13 + h2 * u23)
             h4 = h4 - (h1 * u14 + h2 * u24)
             work[index] = held - ((h1 * u1 + h2 * u2) + (h3 * u3 + h4 * u4))
+        steps_left = max((rank - step) // 4 - 4, 1)
+        for _ in range(-(-len(trail_parts) // steps_left)):
+            trail_parts.pop(0)()
         for n, value in enumerate(done + more):
             if inner + n == 0:
                 final.append(value)
@@ -357,6 +365,8 @@
     size = range_ref.shape[1]
     out_ref[:, :size] = dot_nn(inverse, range_ref[...])
     out_ref[:, size : size + rank] = inverse
+    for copy in trail_copies:
+        copy.wait()
 
 
 def coeff_of(order, basis_ref, selector_ref, coef_ref, piece_refs, stack_ref):
@@ -370,26 +380,32 @@
     return pair_scale(permuted, coef_ref[0:1, :], coef_ref[1:2, :]) / jnp.sqrt(jnp.float32(size))
 
 
-def coeff_kernel(order, basis_ref, other_ref, selector_ref, coef_ref, *refs):
+def coeff_kernel(order, basis_ref, selector_ref, coef_ref, *refs):
+    out_ref, stack_ref = refs[-2:]
+    out_ref[...] = coeff_of(order, basis_ref, selector_ref, coef_ref, refs[:-2], stack_ref)
+
+
+def finish_kernel(order, basis_ref, own_basis_ref, selector_ref, coef_ref, own_ref, *refs):
     core = lax.axis_index("col") % 2
-    basis_out_ref, out_ref, stack_ref, sems = refs[-4:]
+    basis_out_ref, out_ref, stack_ref, result_ref, sems = refs[-5:]
     size = selector_ref.shape[1]
     copies = [
-        pltpu.make_async_copy(source.at[:, :size], basis_out_ref.at[tile], sems.at[n])
-        for n, (source, tile) in enumerate(((basis_ref, core), (other_ref, 1 - core)))
+        pltpu.make_async_copy(source, target, sems.at[n])
+        for n, (source, target) in enumerate(
+            (
+                (own_ref, out_ref.at[core]),
+                (own_basis_ref.at[:, :size], basis_out_ref.at[core]),
+                (basis_ref.at[:, :size], basis_out_ref.at[1 - core]),
+                (result_ref, out_ref.at[1 - core]),
+            )
+        )
     ]
-    for copy in copies:
+    for copy in copies[:3]:
         copy.start()
-    out_ref[...] = coeff_of(order, basis_ref, selector_ref, coef_ref, refs[:-4], stack_ref)
+    result_ref[...] = coeff_of(order, basis_ref, selector_ref, coef_ref, refs[:-5], stack_ref)
+    copies[3].start()
     for copy in copies:
         copy.wait()
-
-
-def finish_kernel(order, basis_ref, selector_ref, coef_ref, own_ref, *refs):
-    core = lax.axis_index("col") % 2
-    out_ref, stack_ref = refs[-2:]
-    out_ref[core] = own_ref[...]
-    out_ref[1 - core] = coeff_of(order, basis_ref, selector_ref, coef_ref, refs[:-2], stack_ref)
 
 
 def dot3(left, right, dims):
@@ -437,38 +453,38 @@
             left_ref[tile, col, :, 2 * rank :] = high[:, part]
 
 
-def trail_kernel(trail_ref, left_ref, right_ref, out_ref, change_ref, held_ref, sems):
+def trail_work(trail_ref, left_ref, right_ref, out_ref, held_ref, sems):
     tiles, ncols, size, _ = left_ref.shape
     groups = right_ref.shape[2] // 128
     step = ncols * groups
     chunks = sems.shape[1]
     rows = size // chunks
-    copies = []
-    for tile in range(tiles):
-        for col in range(ncols):
-            change_ref[col] = jnp.dot(
-                left_ref[tile, col], right_ref[col], preferred_element_type=F32
+    parts, copies = [], []
+
+    def update(tile, chunk, col):
+        change = jnp.dot(
+            left_ref[tile, col, chunk * rows : (chunk + 1) * rows, :],
+            right_ref[col],
+            preferred_element_type=F32,
+        )
+        for group in range(groups):
+            where = pl.ds(chunk * rows * step + col * groups + group, rows, stride=step)
+            held_ref[tile, where, :] = (
+                trail_ref[tile, where, :] - change[:, group * 128 : (group + 1) * 128]
             )
-        for chunk in range(chunks):
-            for col in range(ncols):
-                for group in range(groups):
-                    where = pl.ds(chunk * rows * step + col * groups + group, rows, stride=step)
-                    held_ref[tile, where, :] = (
-                        trail_ref[tile, where, :]
-                        - change_ref[
-                            col,
-                            chunk * rows : (chunk + 1) * rows,
-                            group * 128 : (group + 1) * 128,
-                        ]
-                    )
+        if col == ncols - 1:
             part = pl.ds(chunk * rows * step, rows * step)
             copy = pltpu.make_async_copy(
                 held_ref.at[tile, part], out_ref.at[tile, part], sems.at[tile, chunk]
             )
             copy.start()
             copies.append(copy)
-    for copy in copies:
-        copy.wait()
+
+    for tile in range(tiles):
+        for chunk in range(chunks):
+            for col in range(ncols):
+                parts.append(lambda at=(tile, chunk, col): update(*at))
+    return parts, copies
 
 
 def left_call(nrow, order, tiles, size, factors, cols):
@@ -487,18 +503,17 @@
     )
 
 
-def trail_call(trail, left, right, chunks=4):
+def factor_call(ranges, trail, left, right, chunks=4):
     tiles, _, size, ncols, _, width = trail.shape
-    rows = size * ncols * width // 128
-    view = trail.reshape(tiles, rows, 128)
+    rank = ranges.shape[0]
+    view = trail.reshape(tiles, size * ncols * width // 128, 128)
     vmem = pl.BlockSpec(memory_space=pltpu.VMEM)
-    out = pl.pallas_call(
-        trail_kernel,
-        out_shape=jax.ShapeDtypeStruct(view.shape, F32),
-        in_specs=[vmem] * 3,
-        out_specs=pl.BlockSpec(memory_space=pltpu.HBM),
+    basis, out = pl.pallas_call(
+        factor_kernel,
+        out_shape=[shape(rank, ranges.shape[1] + 128), shape(*view.shape)],
+        in_specs=[vmem] * 4,
+        out_specs=[vmem, pl.BlockSpec(memory_space=pltpu.HBM)],
         scratch_shapes=[
-            pltpu.VMEM((ncols, size, width), F32),
             pltpu.VMEM(view.shape, F32),
             pltpu.SemaphoreType.DMA((tiles, chunks)),
         ],
@@ -508,9 +523,9 @@
             bytes_accessed=2 * view.size * 4,
         ),
         compiler_params=pltpu.CompilerParams(vmem_limit_bytes=20 << 20),
-        name="trail",
-    )(view, left, right)
-    return out.reshape(trail.shape)
+        name="factor",
+    )(ranges, view, left, right)
+    return basis, out.reshape(trail.shape)
 
 
 def body_of(nrow, ncol):
@@ -603,9 +618,9 @@
             near,
             flops=1 << 26,
         )
-        ranges, gram, proj = call(
-            gram_kernel,
-            [shape(rank, size), shape(rank, rank), shape(2, rank, width)],
+        ranges, proj = call(
+            project_kernel,
+            [shape(rank, size), shape(2, rank, width)],
             total,
             remote,
             corr,
@@ -613,35 +628,38 @@
             flops=1 << 26,
         )
         projs = gather(proj, bits[:-1], to_chip)
-        basis = call(factor_kernel, shape(rank, size + 128), gram, ranges, flops=1 << 28)
+        left, right = left_call(nrow, codes(stages(nrow)), 2, size, factors_all, cols)
+        basis, trail_out = factor_call(ranges, trail, left, right)
         basis_other = to_core(basis)
-        left, right = left_call(nrow, codes(stages(nrow)), 2, size, factors_all, cols)
-        trail_out = trail_call(trail, left, right)
         projs_other = []
         for piece in projs:
             projs_other.append(to_core(piece))
         scratch = [pltpu.VMEM((chips, rank, width), F32)]
-        basis_out, coeff = call(
+        coeff = call(
             lambda *refs: coeff_kernel(pair_order, *refs),
-            [shape(2, rank, size), shape(rank, size)],
+            shape(rank, size),
             basis,
-            basis_other,
             selector,
             coef,
             *projs,
-            placed=1,
-            scratch=[*scratch, pltpu.SemaphoreType.DMA((2,))],
+            scratch=scratch,
             flops=1 << 28,
         )
-        coeff_out = call(
+        basis_out, coeff_out = call(
             lambda *refs: finish_kernel(pair_order, *refs),
-            shape(2, rank, size),
+            [shape(2, rank, size)] * 2,
             basis_other,
+            basis,
             selector,
             coef,
             coeff,
             *projs_other,
-            scratch=scratch,
+            placed=2,
+            scratch=[
+                *scratch,
+                pltpu.VMEM((rank, size), F32),
+                pltpu.SemaphoreType.DMA((4,)),
+            ],
             flops=1 << 28,
         )
         return (trail_out, basis_out[:, None], coeff_out[:, None])

time: 46.5 us -> 44.8 us (0.963)
  Pallas kernels: 14.1 us -> 12.5 us
  starting transfers between devices: 11.7 us -> 10.8 us
  waiting for transfers between devices: 19.7 us -> 20.5 us
    pallas_call x12 -> x11, Pallas kernels: 11.4 us -> 7.81 us  [call(): pl.pallas_call(wrapped, out_shape=outs, in_specs=[hbm] * (fetched + kept)...]
    pallas_call x1, Pallas kernels: 2.75 us -> 4.71 us  [factor_call(): pl.pallas_call(factor_kernel, out_shape=[shape(rank, ranges.shape[1] + 12...]
    ppermute x5, starting transfers between devices: 7.48 us -> 6.71 us  [to_chip(): return lax.ppermute(x, 'col', [(i, i ^ 2 * bit) for i in range(ncol)])]
    ppermute x6, waiting for transfers between devices: 0.02 us -> 0.62 us  [to_core(): return lax.ppermute(x, 'col', [(i, i ^ 1) for i in range(ncol)])]
  transfers between devices with their start and end apart: 13 -> 13, of which waited for: 4 -> 5; matrix products, arithmetic and copies ran while one was open for 0% -> 0% of each run, Pallas kernels for 28% -> 13%
where the time goes in v2:
time: 44.8 us; the launch traced here: 44.7 us
  waiting for transfers between devices  20.5 us (46%)
  Pallas kernels  12.5 us (28%)
  starting transfers between devices  10.8 us (24%)
  between operations  0.77 us (2%)
    ppermute x5, waiting for transfers between devices, to_chip(): return lax.ppermute(x, 'col', [(i, i ^ 2 * bit) for i in range(ncol)])  19.9 us
    pallas_call x11, Pallas kernels, call(): pl.pallas_call(wrapped, out_shape=outs, in_specs=[hbm] * (fetched + kept)...  7.81 us
    ppermute x5, starting transfers between devices, to_chip(): return lax.ppermute(x, 'col', [(i, i ^ 2 * bit) for i in range(ncol)])  6.71 us
    pallas_call x1, Pallas kernels, factor_call(): pl.pallas_call(factor_kernel, out_shape=[shape(rank, ranges.shape[1] + 12...  4.71 us
    ppermute x2, starting transfers between devices, to_row(): return lax.ppermute(x, 'row', [(i, i ^ bit) for i in range(nrow)])  3.08 us
    ppermute x6, starting transfers between devices, to_core(): return lax.ppermute(x, 'col', [(i, i ^ 1) for i in range(ncol)])  1.06 us
  transfers between devices with their start and end apart: 13, of which 5 were waited for; matrix products, arithmetic and copies ran while one was open for 0% of the time, Pallas kernels for 13%

profile of v2, /device:TPU:0, one launch (start us, length us, event | category | flops | bytes accessed | tf_op | source)
XLA Modules:
  0.0 44.7 jit_solution(14967140181769603951)
XLA Ops:
  0.6 0.0 copy-start
  0.6 0.6 %collective-permute-start = (f32[2,64,512]{2,1,0:T(8,128)}, f32[2,64,512]{2,1,0:T(8,128)S(1)}, u32[]{:S(2)}, u32[]{:S(2)}) collective-permute-start(f32[2,64,512]{2,1,0:T(8,128)} %bitcast.18), channel_id=1, source_target_pairs={{0,1},{1,0},{2,3},{3,2},{4,5},{5,4},{6,7},{7,6},{8,9},{9,8},{10,11... | collective-permute-start | bytes 786440 | tf_op jit(solution)/shard_map/ppermute | solution.py:536
  1.2 1.6 %shard_map.139 = (f32[1,160,128]{2,1,0:T(8,128)S(1)}, f32[1,256,128]{2,1,0:T(8,128)S(1)}, f32[64,512]{1,0:T(8,128)S(1)}, f32[64,512]{1,0:T(8,128)S(1)}, s32[1,51...) custom-call(f32[2,64,64]{2,1,0:T(8,128)} %bitcast.20, ...), custom_call_target="tpu_custom_call" | custom-call | bytes 1048576 | tf_op jit(solution)/shard_map/pallas_call | solution.py:73
  2.8 3.5 %collective-permute-start.3 = (f32[1,160,128]{2,1,0:T(8,128)S(1)}, f32[1,160,128]{2,1,0:T(8,128)S(1)}, u32[]{:S(2)}, u32[]{:S(2)}) collective-permute-start(f32[1,160,128]{2,1,0:T(8,128)S(1)} %get-tuple-element.32.refs_0_), channel_id=1, source_target_pairs={{0,4},{1,5},{2,6},{3,7},{4,0},{5,1},{6,2},{7,3},{8,12},{9,13},{10,... | collective-permute-start | bytes 245768 | tf_op jit(solution)/shard_map/ppermute | solution.py:539
  6.3 1.5 %collective-permute-start.7 = (f32[1,256,128]{2,1,0:T(8,128)S(1)}, f32[1,256,128]{2,1,0:T(8,128)S(1)}, u32[]{:S(2)}, u32[]{:S(2)}) collective-permute-start(f32[1,256,128]{2,1,0:T(8,128)S(1)} %get-tuple-element.37.refs_0_), channel_id=1, source_target_pairs={{0,16},{8,24},{16,0},{24,8},{1,17},{9,25},{17,1},{25,9},{2,18},{10... | collective-permute-start | bytes 393224 | tf_op jit(solution)/shard_map/ppermute | solution.py:542
  7.8 0.0 collective-permute-done.refs_1_
  7.9 1.6 %collective-permute-start.1 = (f32[128,512]{1,0:T(8,128)S(1)}, f32[128,512]{1,0:T(8,128)S(1)}, u32[]{:S(2)}, u32[]{:S(2)}) collective-permute-start(f32[128,512]{1,0:T(8,128)S(1)} %shard_map.141.refs_1_.refs_6_), channel_id=1, source_target_pairs={{0,2},{1,3},{2,0},{3,1},{4,6},{5,7},{6,4},{7,5},{8,10},{9,11},{10,... | collective-permute-start | bytes 786440 | tf_op jit(solution)/shard_map/ppermute | solution.py:539
  9.5 1.9 %collective-permute-done.3.refs_1_ = f32[1,160,128]{2,1,0:T(8,128)S(1)} collective-permute-done((f32[1,160,128]{2,1,0:T(8,128)S(1)}, f32[1,160,128]{2,1,0:T(8,128)S(1)}, u32[]{:S(2)}, u32[]{:S(2)}) %collective-permute-start.3) | collective-permute-done | bytes 81952 | tf_op jit(solution)/shard_map/ppermute | solution.py:539
  11.5 0.8 %collective-permute-start.4 = (f32[2,160,128]{2,1,0:T(8,128)S(1)}, f32[2,160,128]{2,1,0:T(8,128)S(1)}, u32[]{:S(2)}, u32[]{:S(2)}) collective-permute-start(f32[2,160,128]{2,1,0:T(8,128)S(1)} %shard_map.143.refs_1_), channel_id=1, source_target_pairs={{0,2},{1,3},{2,0},{3,1},{4,6},{5,7},{6,4},{7,5},{8,10},{9,11},{10,... | collective-permute-start | bytes 491528 | tf_op jit(solution)/shard_map/ppermute | solution.py:539
  12.2 0.0 collective-permute-done.7.refs_1_
  12.3 1.6 %collective-permute-start.8 = (f32[2,256,128]{2,1,0:T(8,128)S(1)}, f32[2,256,128]{2,1,0:T(8,128)S(1)}, u32[]{:S(2)}, u32[]{:S(2)}) collective-permute-start(f32[2,256,128]{2,1,0:T(8,128)S(1)} %shard_map.146.refs_1_), channel_id=1, source_target_pairs={{0,8},{8,0},{16,24},{24,16},{1,9},{9,1},{17,25},{25,17},{2,10},{10... | collective-permute-start | bytes 786440 | tf_op jit(solution)/shard_map/ppermute | solution.py:542
  13.8 0.0 collective-permute-start.5
  13.8 6.5 %collective-permute-done.4.refs_2_ = f32[2,160,128]{2,1,0:T(8,128)S(1)} collective-permute-done((f32[2,160,128]{2,1,0:T(8,128)S(1)}, f32[2,160,128]{2,1,0:T(8,128)S(1)}, u32[]{:S(2)}, u32[]{:S(2)}) %collective-permute-start.4) | collective-permute-done | bytes 163872 | tf_op jit(solution)/shard_map/ppermute | solution.py:539
  20.3 0.0 collective-permute-start.6
  20.3 0.6 %shard_map.140 = (f32[4,64,128]{2,1,0:T(8,128)S(1)}, f32[2,512]{1,0:T(2,128)S(1)}, bf16[512,512]{1,0:T(8,128)(2,1)S(1)}) custom-call(f32[64,512]{1,0:T(8,128)S(1)} %get-tuple-element.25.refs_0_, s32[1,512]{1,0:T(1,128)S(1)} %get-tuple-element.26.refs_1_, s32[1,256]{1,0:T(1,128)S(1)} %get-tuple-element.27.refs_2_, f32[3,256]{1,0:T(4,128)S(1)} %get-tuple-element.28.refs_3_), custom_call_target="tpu_custom_call" | custom-call | flops 268435456 | bytes 1048576 | tf_op jit(solution)/shard_map/pallas_call | solution.py:73
  20.9 0.0 collective-permute-done.1.refs_2_.refs_7_
  20.9 0.4 shard_map.142.refs_0_
  21.3 0.7 %collective-permute-start.2 = (f32[64,512]{1,0:T(8,128)S(1)}, f32[64,512]{1,0:T(8,128)S(1)}, u32[]{:S(2)}, u32[]{:S(2)}) collective-permute-start(f32[64,512]{1,0:T(8,128)S(1)} %shard_map.142.refs_0_), channel_id=1, source_target_pairs={{0,4},{1,5},{2,6},{3,7},{4,0},{5,1},{6,2},{7,3},{8,12},{9,13},{10,... | collective-permute-start | bytes 393224 | tf_op jit(solution)/shard_map/ppermute | solution.py:539
  22.0 0.0 collective-permute-done.5.refs_3_
  22.0 0.0 collective-permute-done.6.refs_4_
  22.0 1.5 %shard_map.144 = (f32[4,2,160,128]{3,2,1,0:T(8,128)S(1)}, f32[64,512]{1,0:T(8,128)S(1)}, f32[2,128,512]{2,1,0:T(8,128)S(1)}) custom-call(f32[64,512]{1,0:T(8,128)S(1)} %get-tuple-element.31.refs_0_, f32[2,160,128]{2,1,0:T(8,128)S(1)} %shard_map.143.refs_1_, f32[2,160,128]{2,1,0:T(8,128)S(1)} %collective-permute-done.4.refs_2_, ...), custom_call_target="tpu_custom_call" | custom-call | flops 67108864 | bytes 1048576 | tf_op jit(solution)/shard_map/pallas_call | solution.py:73
  23.5 0.0 collective-permute-done.8.refs_2_
  23.5 1.2 %shard_map.147 = (bf16[2,2,512,192]{3,2,1,0:T(8,128)(2,1)S(1)}, bf16[2,192,512]{2,1,0:T(8,128)(2,1)S(1)}) custom-call(f32[4,2,160,128]{3,2,1,0:T(8,128)S(1)} %get-tuple-element.36.refs_0_, f32[2,256,128]{2,1,0:T(8,128)S(1)} %shard_map.146.refs_1_, f32[2,256,128]{2,1,0:T(8,128)S(1)} %collective-permute-done.8.refs_2_), custom_call_target="tpu_custom_call" | custom-call | flops 67108864 | bytes 1048576 | tf_op jit(solution)/shard_map/pallas_call | solution.py:73
  24.7 6.3 %collective-permute-done.2.refs_1_ = f32[64,512]{1,0:T(8,128)S(1)} collective-permute-done((f32[64,512]{1,0:T(8,128)S(1)}, f32[64,512]{1,0:T(8,128)S(1)}, u32[]{:S(2)}, u32[]{:S(2)}) %collective-permute-start.2) | collective-permute-done | bytes 131104 | tf_op jit(solution)/shard_map/ppermute | solution.py:539
  31.0 0.6 %shard_map.145 = (f32[64,512]{1,0:T(8,128)S(1)}, f32[2,64,128]{2,1,0:T(8,128)S(1)}) custom-call(f32[64,512]{1,0:T(8,128)S(1)} %shard_map.142.refs_0_, f32[64,512]{1,0:T(8,128)S(1)} %collective-permute-done.2.refs_1_, f32[64,512]{1,0:T(8,128)S(1)} %get-tuple-element.33.refs_2_, f32[2,128,512]{2,1,0:T(8,128)S(1)} %get-tuple-element.34.refs_3_), custom_call_target="tpu_custom_call" | custom-call | flops 67108864 | bytes 1048576 | tf_op jit(solution)/shard_map/pallas_call | solution.py:73
  31.6 0.0 copy-done
  31.6 4.7 %factor.1 = (f32[64,640]{1,0:T(8,128)S(1)}, f32[2,4096,128]{2,1,0:T(8,128)}) custom-call(f32[64,512]{1,0:T(8,128)S(1)} %get-tuple-element.35.range_ref, f32[2,4096,128]{2,1,0:T(8,128)S(1)} %bitcast.17, bf16[2,2,512,192]{3,2,1,0:T(8,128)(2,1)S(1)} %get-tuple-element.38.left_ref, bf16[2,192,512]{2,1,0:T(8,128)(2,1)S(1)} %get-tuple-element.39.right_ref), custom_call_target="tpu_custom_call" | custom-call | flops 402653184 | bytes 8388608 | tf_op jit(solution)/shard_map/factor/pallas_call | solution.py:511
  36.3 0.1 collective-permute-start.9
  36.4 0.1 collective-permute-start.10
  36.5 0.4 collective-permute-start.11
  36.9 5.2 %collective-permute-done.10.refs_4_ = f32[2,64,128]{2,1,0:T(8,128)S(1)} collective-permute-done((f32[2,64,128]{2,1,0:T(8,128)S(1)}, f32[2,64,128]{2,1,0:T(8,128)S(1)}, u32[]{:S(2)}, u32[]{:S(2)}) %collective-permute-start.10) | collective-permute-done | bytes 65568 | tf_op jit(solution)/shard_map/ppermute | solution.py:539
  42.1 0.0 collective-permute-start.12
  42.1 0.6 %shard_map.148.refs_4_ = f32[64,512]{1,0:T(8,128)S(1)} custom-call(f32[64,640]{1,0:T(8,128)S(1)} %get-tuple-element.41.refs_0_.refs_1_, bf16[512,512]{1,0:T(8,128)(2,1)S(1)} %get-tuple-element.42.refs_1_.refs_2_, f32[2,512]{1,0:T(2,128)S(1)} %get-tuple-element.43.refs_2_.refs_3_, f32[2,64,128]{2,1,0:T(8,128)S(1)} %get-tuple-element.44.refs_3_, ...), custom_call_target="tpu_custom_call" | custom-call | flops 268435456 | bytes 1048576 | tf_op jit(solution)/shard_map/pallas_call | solution.py:73
  42.7 0.0 collective-permute-done.11.refs_5_
  42.7 0.6 %collective-permute-done.12.refs_6_ = f32[2,64,128]{2,1,0:T(8,128)S(1)} collective-permute-done((f32[2,64,128]{2,1,0:T(8,128)S(1)}, f32[2,64,128]{2,1,0:T(8,128)S(1)}, u32[]{:S(2)}, u32[]{:S(2)}) %collective-permute-start.12) | collective-permute-done | bytes 65568 | tf_op jit(solution)/shard_map/ppermute | solution.py:536
  43.3 0.0 collective-permute-done.9.refs_0_
  43.3 1.3 %shard_map.149 = (f32[2,64,512]{2,1,0:T(8,128)}, f32[2,64,512]{2,1,0:T(8,128)}) custom-call(f32[64,640]{1,0:T(8,128)S(1)} %collective-permute-done.9.refs_0_, f32[64,640]{1,0:T(8,128)S(1)} %get-tuple-element.41.refs_0_.refs_1_, bf16[512,512]{1,0:T(8,128)(2,1)S(1)} %get-tuple-element.42.refs_1_.refs_2_, f32[2,512]{1,0:T(2,128)S(1)} %get-tuple-element.43.refs_2_.refs_3_, ...), custom_call_target="tpu_custom_call" | custom-call | flops 268435456 | bytes 1048576 | tf_op jit(solution)/shard_map/pallas_call | solution.py:73
  (3 shorter events, 0.1 us)
Async XLA Ops:
  0.6 30.9 %copy-start = (f32[2,1,512,2,1,512]{5,4,3,2,1,0:T(1,128)S(1)}, f32[2,1,512,2,1,512]{5,4,3,2,1,0:T(1,128)}, u32[]{:S(2)}) copy-start(f32[2,1,512,2,1,512]{5,4,3,2,1,0:T(1,128)} %param.12) | copy-start | bytes 12582916
  0.6 7.2 %collective-permute-start = (f32[2,64,512]{2,1,0:T(8,128)}, f32[2,64,512]{2,1,0:T(8,128)S(1)}, u32[]{:S(2)}, u32[]{:S(2)}) collective-permute-start(f32[2,64,512]{2,1,0:T(8,128)} %bitcast.18), channel_id=1, source_target_pairs={{0,1},{1,0},{2,3},{3,2},{4,5},{5,4},{6,7},{7,6},{8,9},{9,8},{10,11... | collective-permute-start | bytes 786440 | tf_op jit(solution)/shard_map/ppermute | solution.py:536
  2.8 8.7 %collective-permute-start.3 = (f32[1,160,128]{2,1,0:T(8,128)S(1)}, f32[1,160,128]{2,1,0:T(8,128)S(1)}, u32[]{:S(2)}, u32[]{:S(2)}) collective-permute-start(f32[1,160,128]{2,1,0:T(8,128)S(1)} %get-tuple-element.32.refs_0_), channel_id=1, source_target_pairs={{0,4},{1,5},{2,6},{3,7},{4,0},{5,1},{6,2},{7,3},{8,12},{9,13},{10,... | collective-permute-start | bytes 245768 | tf_op jit(solution)/shard_map/ppermute | solution.py:539
  6.3 5.9 %collective-permute-start.7 = (f32[1,256,128]{2,1,0:T(8,128)S(1)}, f32[1,256,128]{2,1,0:T(8,128)S(1)}, u32[]{:S(2)}, u32[]{:S(2)}) collective-permute-start(f32[1,256,128]{2,1,0:T(8,128)S(1)} %get-tuple-element.37.refs_0_), channel_id=1, source_target_pairs={{0,16},{8,24},{16,0},{24,8},{1,17},{9,25},{17,1},{25,9},{2,18},{10... | collective-permute-start | bytes 393224 | tf_op jit(solution)/shard_map/ppermute | solution.py:542
  7.9 13.1 %collective-permute-start.1 = (f32[128,512]{1,0:T(8,128)S(1)}, f32[128,512]{1,0:T(8,128)S(1)}, u32[]{:S(2)}, u32[]{:S(2)}) collective-permute-start(f32[128,512]{1,0:T(8,128)S(1)} %shard_map.141.refs_1_.refs_6_), channel_id=1, source_target_pairs={{0,2},{1,3},{2,0},{3,1},{4,6},{5,7},{6,4},{7,5},{8,10},{9,11},{10,... | collective-permute-start | bytes 786440 | tf_op jit(solution)/shard_map/ppermute | solution.py:539
  11.5 8.9 %collective-permute-start.4 = (f32[2,160,128]{2,1,0:T(8,128)S(1)}, f32[2,160,128]{2,1,0:T(8,128)S(1)}, u32[]{:S(2)}, u32[]{:S(2)}) collective-permute-start(f32[2,160,128]{2,1,0:T(8,128)S(1)} %shard_map.143.refs_1_), channel_id=1, source_target_pairs={{0,2},{1,3},{2,0},{3,1},{4,6},{5,7},{6,4},{7,5},{8,10},{9,11},{10,... | collective-permute-start | bytes 491528 | tf_op jit(solution)/shard_map/ppermute | solution.py:539
  12.3 11.3 %collective-permute-start.8 = (f32[2,256,128]{2,1,0:T(8,128)S(1)}, f32[2,256,128]{2,1,0:T(8,128)S(1)}, u32[]{:S(2)}, u32[]{:S(2)}) collective-permute-start(f32[2,256,128]{2,1,0:T(8,128)S(1)} %shard_map.146.refs_1_), channel_id=1, source_target_pairs={{0,8},{8,0},{16,24},{24,16},{1,9},{9,1},{17,25},{25,17},{2,10},{10... | collective-permute-start | bytes 786440 | tf_op jit(solution)/shard_map/ppermute | solution.py:542
  13.8 8.2 %collective-permute-start.5 = (f32[2,160,128]{2,1,0:T(8,128)S(1)}, f32[2,160,128]{2,1,0:T(8,128)S(1)}, u32[]{:S(2)}, u32[]{:S(2)}) collective-permute-start(f32[2,160,128]{2,1,0:T(8,128)S(1)} %shard_map.143.refs_1_), channel_id=1, source_target_pairs={{0,1},{1,0},{2,3},{3,2},{4,5},{5,4},{6,7},{7,6},{8,9},{9,8},{10,11... | collective-permute-start | bytes 491528 | tf_op jit(solution)/shard_map/ppermute | solution.py:536
  20.3 1.7 %collective-permute-start.6 = (f32[2,160,128]{2,1,0:T(8,128)S(1)}, f32[2,160,128]{2,1,0:T(8,128)S(1)}, u32[]{:S(2)}, u32[]{:S(2)}) collective-permute-start(f32[2,160,128]{2,1,0:T(8,128)S(1)} %collective-permute-done.4.refs_2_), channel_id=1, source_target_pairs={{0,1},{1,0},{2,3},{3,2},{4,5},{5,4},{6,7},{7,6},{8,9},{9,8},{10,11... | collective-permute-start | bytes 491528 | tf_op jit(solution)/shard_map/ppermute | solution.py:536
  21.3 9.7 %collective-permute-start.2 = (f32[64,512]{1,0:T(8,128)S(1)}, f32[64,512]{1,0:T(8,128)S(1)}, u32[]{:S(2)}, u32[]{:S(2)}) collective-permute-start(f32[64,512]{1,0:T(8,128)S(1)} %shard_map.142.refs_0_), channel_id=1, source_target_pairs={{0,4},{1,5},{2,6},{3,7},{4,0},{5,1},{6,2},{7,3},{8,12},{9,13},{10,... | collective-permute-start | bytes 393224 | tf_op jit(solution)/shard_map/ppermute | solution.py:539
  36.3 7.0 %collective-permute-start.9 = (f32[64,640]{1,0:T(8,128)S(1)}, f32[64,640]{1,0:T(8,128)S(1)}, u32[]{:S(2)}, u32[]{:S(2)}) collective-permute-start(f32[64,640]{1,0:T(8,128)S(1)} %get-tuple-element.41.refs_0_.refs_1_), channel_id=1, source_target_pairs={{0,1},{1,0},{2,3},{3,2},{4,5},{5,4},{6,7},{7,6},{8,9},{9,8},{10,11... | collective-permute-start | bytes 491528 | tf_op jit(solution)/shard_map/ppermute | solution.py:536
  36.4 5.7 %collective-permute-start.10 = (f32[2,64,128]{2,1,0:T(8,128)S(1)}, f32[2,64,128]{2,1,0:T(8,128)S(1)}, u32[]{:S(2)}, u32[]{:S(2)}) collective-permute-start(f32[2,64,128]{2,1,0:T(8,128)S(1)} %get-tuple-element.44.refs_3_), channel_id=1, source_target_pairs={{0,4},{1,5},{2,6},{3,7},{4,0},{5,1},{6,2},{7,3},{8,12},{9,13},{10,... | collective-permute-start | bytes 196616 | tf_op jit(solution)/shard_map/ppermute | solution.py:539
  36.5 6.2 %collective-permute-start.11 = (f32[2,64,128]{2,1,0:T(8,128)S(1)}, f32[2,64,128]{2,1,0:T(8,128)S(1)}, u32[]{:S(2)}, u32[]{:S(2)}) collective-permute-start(f32[2,64,128]{2,1,0:T(8,128)S(1)} %get-tuple-element.44.refs_3_), channel_id=1, source_target_pairs={{0,1},{1,0},{2,3},{3,2},{4,5},{5,4},{6,7},{7,6},{8,9},{9,8},{10,11... | collective-permute-start | bytes 196616 | tf_op jit(solution)/shard_map/ppermute | solution.py:536
  42.1 1.3 %collective-permute-start.12 = (f32[2,64,128]{2,1,0:T(8,128)S(1)}, f32[2,64,128]{2,1,0:T(8,128)S(1)}, u32[]{:S(2)}, u32[]{:S(2)}) collective-permute-start(f32[2,64,128]{2,1,0:T(8,128)S(1)} %collective-permute-done.10.refs_4_), channel_id=1, source_target_pairs={{0,1},{1,0},{2,3},{3,2},{4,5},{5,4},{6,7},{7,6},{8,9},{9,8},{10,11... | collective-permute-start | bytes 196616 | tf_op jit(solution)/shard_map/ppermute | solution.py:536

commit v3 on v2

--- a/solution.py
+++ b/solution.py
@@ -9,6 +9,8 @@
 F32 = jnp.float32
 BF16 = jnp.bfloat16
 HIGHEST = lax.Precision.HIGHEST
+NN = ((1,), (0,))
+NT = ((1,), (1,))
 
 
 def dot_nn(left, right):
@@ -21,6 +23,51 @@
     return lax.dot_general(
         left, right, (((1,), (1,)), ((), ())), precision=HIGHEST, preferred_element_type=F32
     )
+
+
+def dot3(left, right, dims):
+    high = left.astype(BF16)
+    low = (left - high.astype(F32)).astype(BF16)
+    top = right.astype(BF16)
+    rest = (right - top.astype(F32)).astype(BF16)
+    dot = lambda a, b: lax.dot_general(a, b, (dims, ((), ())), preferred_element_type=F32)
+    return dot(high, top) + (dot(low, top) + dot(high, rest))
+
+
+def left_kernel(order, factors_ref, *refs):
+    col_refs, (left_ref, right_ref, cols_ref) = refs[:-3], refs[-3:]
+    row = lax.axis_index("row")
+    tiles, ncols, _, deep = left_ref.shape
+    rank = deep // 3
+    for code, ref, t in entries(col_refs, order):
+        cols_ref[row ^ code] = ref[t]
+    for col in range(ncols):
+        basis = lanes(cols_ref, 2 * col * rank, (2 * col + 1) * rank)
+        high = basis.astype(BF16)
+        right_ref[col, :rank, :] = high
+        right_ref[col, rank : 2 * rank, :] = high
+        right_ref[col, 2 * rank :, :] = (basis - high.astype(F32)).astype(BF16)
+    scaled = jnp.concatenate(
+        [lanes(cols_ref, (2 * col + 1) * rank, (2 * col + 2) * rank) for col in range(ncols)],
+        axis=0,
+    )
+    yrows = jnp.concatenate(
+        [lanes(factors_ref, tile, rank, 2 * rank) for tile in range(tiles)], axis=0
+    )
+    core = dot3(scaled, yrows, ((1,), (1,)))
+    for tile in range(tiles):
+        left = dot3(
+            core[:, tile * rank : (tile + 1) * rank],
+            lanes(factors_ref, tile, 0, rank),
+            ((1,), (0,)),
+        ).T
+        high = left.astype(BF16)
+        low = (left - high.astype(F32)).astype(BF16)
+        for col in range(ncols):
+            part = slice(col * rank, (col + 1) * rank)
+            left_ref[tile, col, :, :rank] = high[:, part]
+            left_ref[tile, col, :, rank : 2 * rank] = low[:, part]
+            left_ref[tile, col, :, 2 * rank :] = high[:, part]
 
 
 def split3(x):
@@ -257,8 +304,8 @@
     pbasis = jnp.concatenate(
         [lanes(factors_ref, tile, 2 * rank, 2 * rank + rank // 2) for tile in range(2)], axis=0
     )
-    pcore = dot_nt(yrow, pivot_ref[...])
-    mixed = dot_nt(dot_nt(lanes(sketch_ref, 0, rank), pbasis), pcore)
+    pcore = dot3(yrow, pivot_ref[...], NT)
+    mixed = dot3(dot3(lanes(sketch_ref, 0, rank), pbasis, NT), pcore, NT)
     local = jnp.concatenate(
         [
             jnp.concatenate(
@@ -272,8 +319,8 @@
         ],
         axis=1,
     )
-    sides = jnp.concatenate([mixed, dot_nn(pcore, local).T], axis=0)
-    change = dot_nn(sides, xrow)
+    sides = jnp.concatenate([mixed, dot3(pcore, local, NN).T], axis=0)
+    change = dot3(sides, xrow, NN)
     corr_ref[...] = change[:rank]
     at = rank
     for slot, panel_ref in enumerate(panel_refs):
@@ -406,51 +453,6 @@
     copies[3].start()
     for copy in copies:
         copy.wait()
-
-
-def dot3(left, right, dims):
-    high, low = left.astype(BF16), None
-    low = (left - high.astype(F32)).astype(BF16)
-    top = right.astype(BF16)
-    rest = (right - top.astype(F32)).astype(BF16)
-    dot = lambda a, b: lax.dot_general(a, b, (dims, ((), ())), preferred_element_type=F32)
-    return dot(high, top) + (dot(low, top) + dot(high, rest))
-
-
-def left_kernel(order, factors_ref, *refs):
-    col_refs, (left_ref, right_ref, cols_ref) = refs[:-3], refs[-3:]
-    row = lax.axis_index("row")
-    tiles, ncols, _, deep = left_ref.shape
-    rank = deep // 3
-    for code, ref, t in entries(col_refs, order):
-        cols_ref[row ^ code] = ref[t]
-    for col in range(ncols):
-        basis = lanes(cols_ref, 2 * col * rank, (2 * col + 1) * rank)
-        high = basis.astype(BF16)
-        right_ref[col, :rank, :] = high
-        right_ref[col, rank : 2 * rank, :] = high
-        right_ref[col, 2 * rank :, :] = (basis - high.astype(F32)).astype(BF16)
-    scaled = jnp.concatenate(
-        [lanes(cols_ref, (2 * col + 1) * rank, (2 * col + 2) * rank) for col in range(ncols)],
-        axis=0,
-    )
-    yrows = jnp.concatenate(
-        [lanes(factors_ref, tile, rank, 2 * rank) for tile in range(tiles)], axis=0
-    )
-    core = dot3(scaled, yrows, ((1,), (1,)))
-    for tile in range(tiles):
-        left = dot3(
-            core[:, tile * rank : (tile + 1) * rank],
-            lanes(factors_ref, tile, 0, rank),
-            ((1,), (0,)),
-        ).T
-        high = left.astype(BF16)
-        low = (left - high.astype(F32)).astype(BF16)
-        for col in range(ncols):
-            part = slice(col * rank, (col + 1) * rank)
-            left_ref[tile, col, :, :rank] = high[:, part]
-            left_ref[tile, col, :, rank : 2 * rank] = low[:, part]
-            left_ref[tile, col, :, 2 * rank :] = high[:, part]
 
 
 def trail_work(trail_ref, left_ref, right_ref, out_ref, held_ref, sems):

time: 44.8 us -> 44.8 us (level)
  waiting for transfers between devices: 20.5 us -> 21 us
    ppermute x5, waiting for transfers between devices: 19.9 us -> 20.4 us  [to_chip(): return lax.ppermute(x, 'col', [(i, i ^ 2 * bit) for i in range(ncol)])]
    pallas_call x11, Pallas kernels: 7.81 us -> 7.35 us  [call(): pl.pallas_call(wrapped, out_shape=outs, in_specs=[hbm] * (fetched + kept)...]
  transfers between devices with their start and end apart: 13 -> 13, of which waited for: 5 -> 5; matrix products, arithmetic and copies ran while one was open for 0% -> 0% of each run, Pallas kernels for 13% -> 12%
where the time goes in v3:
time: 44.8 us; the launch traced here: 44.7 us
  waiting for transfers between devices  21 us (47%)
  Pallas kernels  12.1 us (27%)
  starting transfers between devices  10.8 us (24%)
  between operations  0.77 us (2%)
    ppermute x5, waiting for transfers between devices, to_chip(): return lax.ppermute(x, 'col', [(i, i ^ 2 * bit) for i in range(ncol)])  20.4 us
    pallas_call x11, Pallas kernels, call(): pl.pallas_call(wrapped, out_shape=outs, in_specs=[hbm] * (fetched + kept)...  7.35 us
    ppermute x5, starting transfers between devices, to_chip(): return lax.ppermute(x, 'col', [(i, i ^ 2 * bit) for i in range(ncol)])  6.71 us
    pallas_call x1, Pallas kernels, factor_call(): pl.pallas_call(factor_kernel, out_shape=[shape(rank, ranges.shape[1] + 12...  4.71 us
    ppermute x2, starting transfers between devices, to_row(): return lax.ppermute(x, 'row', [(i, i ^ bit) for i in range(nrow)])  3.08 us
    ppermute x6, starting transfers between devices, to_core(): return lax.ppermute(x, 'col', [(i, i ^ 1) for i in range(ncol)])  1.06 us
  transfers between devices with their start and end apart: 13, of which 5 were waited for; matrix products, arithmetic and copies ran while one was open for 0% of the time, Pallas kernels for 12%

profile of v3, /device:TPU:0, one launch (start us, length us, event | category | flops | bytes accessed | tf_op | source)
XLA Modules:
  0.0 44.7 jit_solution(3972048953466930330)
XLA Ops:
  0.6 0.0 copy-start
  0.6 0.6 %collective-permute-start = (f32[2,64,512]{2,1,0:T(8,128)}, f32[2,64,512]{2,1,0:T(8,128)S(1)}, u32[]{:S(2)}, u32[]{:S(2)}) collective-permute-start(f32[2,64,512]{2,1,0:T(8,128)} %bitcast.18), channel_id=1, source_target_pairs={{0,1},{1,0},{2,3},{3,2},{4,5},{5,4},{6,7},{7,6},{8,9},{9,8},{10,11... | collective-permute-start | bytes 786440 | tf_op jit(solution)/shard_map/ppermute | solution.py:538
  1.2 1.6 %shard_map.139 = (f32[1,160,128]{2,1,0:T(8,128)S(1)}, f32[1,256,128]{2,1,0:T(8,128)S(1)}, f32[64,512]{1,0:T(8,128)S(1)}, f32[64,512]{1,0:T(8,128)S(1)}, s32[1,51...) custom-call(f32[2,64,64]{2,1,0:T(8,128)} %bitcast.20, ...), custom_call_target="tpu_custom_call" | custom-call | bytes 1048576 | tf_op jit(solution)/shard_map/pallas_call | solution.py:120
  2.8 3.5 %collective-permute-start.3 = (f32[1,160,128]{2,1,0:T(8,128)S(1)}, f32[1,160,128]{2,1,0:T(8,128)S(1)}, u32[]{:S(2)}, u32[]{:S(2)}) collective-permute-start(f32[1,160,128]{2,1,0:T(8,128)S(1)} %get-tuple-element.32.refs_0_), channel_id=1, source_target_pairs={{0,4},{1,5},{2,6},{3,7},{4,0},{5,1},{6,2},{7,3},{8,12},{9,13},{10,... | collective-permute-start | bytes 245768 | tf_op jit(solution)/shard_map/ppermute | solution.py:541
  6.3 1.5 %collective-permute-start.7 = (f32[1,256,128]{2,1,0:T(8,128)S(1)}, f32[1,256,128]{2,1,0:T(8,128)S(1)}, u32[]{:S(2)}, u32[]{:S(2)}) collective-permute-start(f32[1,256,128]{2,1,0:T(8,128)S(1)} %get-tuple-element.37.refs_0_), channel_id=1, source_target_pairs={{0,16},{8,24},{16,0},{24,8},{1,17},{9,25},{17,1},{25,9},{2,18},{10... | collective-permute-start | bytes 393224 | tf_op jit(solution)/shard_map/ppermute | solution.py:544
  7.8 0.0 collective-permute-done.refs_1_
  7.9 1.6 %collective-permute-start.1 = (f32[128,512]{1,0:T(8,128)S(1)}, f32[128,512]{1,0:T(8,128)S(1)}, u32[]{:S(2)}, u32[]{:S(2)}) collective-permute-start(f32[128,512]{1,0:T(8,128)S(1)} %shard_map.141.refs_1_.refs_6_), channel_id=1, source_target_pairs={{0,2},{1,3},{2,0},{3,1},{4,6},{5,7},{6,4},{7,5},{8,10},{9,11},{10,... | collective-permute-start | bytes 786440 | tf_op jit(solution)/shard_map/ppermute | solution.py:541
  9.5 1.9 %collective-permute-done.3.refs_1_ = f32[1,160,128]{2,1,0:T(8,128)S(1)} collective-permute-done((f32[1,160,128]{2,1,0:T(8,128)S(1)}, f32[1,160,128]{2,1,0:T(8,128)S(1)}, u32[]{:S(2)}, u32[]{:S(2)}) %collective-permute-start.3) | collective-permute-done | bytes 81952 | tf_op jit(solution)/shard_map/ppermute | solution.py:541
  11.5 0.8 %collective-permute-start.4 = (f32[2,160,128]{2,1,0:T(8,128)S(1)}, f32[2,160,128]{2,1,0:T(8,128)S(1)}, u32[]{:S(2)}, u32[]{:S(2)}) collective-permute-start(f32[2,160,128]{2,1,0:T(8,128)S(1)} %shard_map.143.refs_1_), channel_id=1, source_target_pairs={{0,2},{1,3},{2,0},{3,1},{4,6},{5,7},{6,4},{7,5},{8,10},{9,11},{10,... | collective-permute-start | bytes 491528 | tf_op jit(solution)/shard_map/ppermute | solution.py:541
  12.2 0.0 collective-permute-done.7.refs_1_
  12.3 1.6 %collective-permute-start.8 = (f32[2,256,128]{2,1,0:T(8,128)S(1)}, f32[2,256,128]{2,1,0:T(8,128)S(1)}, u32[]{:S(2)}, u32[]{:S(2)}) collective-permute-start(f32[2,256,128]{2,1,0:T(8,128)S(1)} %shard_map.146.refs_1_), channel_id=1, source_target_pairs={{0,8},{8,0},{16,24},{24,16},{1,9},{9,1},{17,25},{25,17},{2,10},{10... | collective-permute-start | bytes 786440 | tf_op jit(solution)/shard_map/ppermute | solution.py:544
  13.8 0.0 collective-permute-start.5
  13.8 6.5 %collective-permute-done.4.refs_2_ = f32[2,160,128]{2,1,0:T(8,128)S(1)} collective-permute-done((f32[2,160,128]{2,1,0:T(8,128)S(1)}, f32[2,160,128]{2,1,0:T(8,128)S(1)}, u32[]{:S(2)}, u32[]{:S(2)}) %collective-permute-start.4) | collective-permute-done | bytes 163872 | tf_op jit(solution)/shard_map/ppermute | solution.py:541
  20.3 0.0 collective-permute-start.6
  20.3 0.6 %shard_map.140 = (f32[4,64,128]{2,1,0:T(8,128)S(1)}, f32[2,512]{1,0:T(2,128)S(1)}, bf16[512,512]{1,0:T(8,128)(2,1)S(1)}) custom-call(f32[64,512]{1,0:T(8,128)S(1)} %get-tuple-element.25.refs_0_, s32[1,512]{1,0:T(1,128)S(1)} %get-tuple-element.26.refs_1_, s32[1,256]{1,0:T(1,128)S(1)} %get-tuple-element.27.refs_2_, f32[3,256]{1,0:T(4,128)S(1)} %get-tuple-element.28.refs_3_), custom_call_target="tpu_custom_call" | custom-call | flops 268435456 | bytes 1048576 | tf_op jit(solution)/shard_map/pallas_call | solution.py:120
  20.9 0.0 collective-permute-done.1.refs_2_.refs_7_
  20.9 0.4 shard_map.142.refs_0_
  21.3 0.7 %collective-permute-start.2 = (f32[64,512]{1,0:T(8,128)S(1)}, f32[64,512]{1,0:T(8,128)S(1)}, u32[]{:S(2)}, u32[]{:S(2)}) collective-permute-start(f32[64,512]{1,0:T(8,128)S(1)} %shard_map.142.refs_0_), channel_id=1, source_target_pairs={{0,4},{1,5},{2,6},{3,7},{4,0},{5,1},{6,2},{7,3},{8,12},{9,13},{10,... | collective-permute-start | bytes 393224 | tf_op jit(solution)/shard_map/ppermute | solution.py:541
  22.0 0.0 collective-permute-done.5.refs_3_
  22.0 0.0 collective-permute-done.6.refs_4_
  22.0 1.1 %shard_map.144 = (f32[4,2,160,128]{3,2,1,0:T(8,128)S(1)}, f32[64,512]{1,0:T(8,128)S(1)}, f32[2,128,512]{2,1,0:T(8,128)S(1)}) custom-call(f32[64,512]{1,0:T(8,128)S(1)} %get-tuple-element.31.refs_0_, f32[2,160,128]{2,1,0:T(8,128)S(1)} %shard_map.143.refs_1_, f32[2,160,128]{2,1,0:T(8,128)S(1)} %collective-permute-done.4.refs_2_, ...), custom_call_target="tpu_custom_call" | custom-call | flops 67108864 | bytes 1048576 | tf_op jit(solution)/shard_map/pallas_call | solution.py:120
  23.1 0.0 collective-permute-done.8.refs_2_
  23.1 1.2 %shard_map.147 = (bf16[2,2,512,192]{3,2,1,0:T(8,128)(2,1)S(1)}, bf16[2,192,512]{2,1,0:T(8,128)(2,1)S(1)}) custom-call(f32[4,2,160,128]{3,2,1,0:T(8,128)S(1)} %get-tuple-element.36.refs_0_, f32[2,256,128]{2,1,0:T(8,128)S(1)} %shard_map.146.refs_1_, f32[2,256,128]{2,1,0:T(8,128)S(1)} %collective-permute-done.8.refs_2_), custom_call_target="tpu_custom_call" | custom-call | flops 67108864 | bytes 1048576 | tf_op jit(solution)/shard_map/pallas_call | solution.py:120
  24.3 6.7 %collective-permute-done.2.refs_1_ = f32[64,512]{1,0:T(8,128)S(1)} collective-permute-done((f32[64,512]{1,0:T(8,128)S(1)}, f32[64,512]{1,0:T(8,128)S(1)}, u32[]{:S(2)}, u32[]{:S(2)}) %collective-permute-start.2) | collective-permute-done | bytes 131104 | tf_op jit(solution)/shard_map/ppermute | solution.py:541
  31.0 0.6 %shard_map.145 = (f32[64,512]{1,0:T(8,128)S(1)}, f32[2,64,128]{2,1,0:T(8,128)S(1)}) custom-call(f32[64,512]{1,0:T(8,128)S(1)} %shard_map.142.refs_0_, f32[64,512]{1,0:T(8,128)S(1)} %collective-permute-done.2.refs_1_, f32[64,512]{1,0:T(8,128)S(1)} %get-tuple-element.33.refs_2_, f32[2,128,512]{2,1,0:T(8,128)S(1)} %get-tuple-element.34.refs_3_), custom_call_target="tpu_custom_call" | custom-call | flops 67108864 | bytes 1048576 | tf_op jit(solution)/shard_map/pallas_call | solution.py:120
  31.6 0.0 copy-done
  31.6 4.7 %factor.1 = (f32[64,640]{1,0:T(8,128)S(1)}, f32[2,4096,128]{2,1,0:T(8,128)}) custom-call(f32[64,512]{1,0:T(8,128)S(1)} %get-tuple-element.35.range_ref, f32[2,4096,128]{2,1,0:T(8,128)S(1)} %bitcast.17, bf16[2,2,512,192]{3,2,1,0:T(8,128)(2,1)S(1)} %get-tuple-element.38.left_ref, bf16[2,192,512]{2,1,0:T(8,128)(2,1)S(1)} %get-tuple-element.39.right_ref), custom_call_target="tpu_custom_call" | custom-call | flops 402653184 | bytes 8388608 | tf_op jit(solution)/shard_map/factor/pallas_call | solution.py:513
  36.3 0.1 collective-permute-start.9
  36.4 0.1 collective-permute-start.10
  36.5 0.4 collective-permute-start.11
  36.9 5.2 %collective-permute-done.10.refs_4_ = f32[2,64,128]{2,1,0:T(8,128)S(1)} collective-permute-done((f32[2,64,128]{2,1,0:T(8,128)S(1)}, f32[2,64,128]{2,1,0:T(8,128)S(1)}, u32[]{:S(2)}, u32[]{:S(2)}) %collective-permute-start.10) | collective-permute-done | bytes 65568 | tf_op jit(solution)/shard_map/ppermute | solution.py:541
  42.1 0.0 collective-permute-start.12
  42.1 0.6 %shard_map.148.refs_4_ = f32[64,512]{1,0:T(8,128)S(1)} custom-call(f32[64,640]{1,0:T(8,128)S(1)} %get-tuple-element.41.refs_0_.refs_1_, bf16[512,512]{1,0:T(8,128)(2,1)S(1)} %get-tuple-element.42.refs_1_.refs_2_, f32[2,512]{1,0:T(2,128)S(1)} %get-tuple-element.43.refs_2_.refs_3_, f32[2,64,128]{2,1,0:T(8,128)S(1)} %get-tuple-element.44.refs_3_, ...), custom_call_target="tpu_custom_call" | custom-call | flops 268435456 | bytes 1048576 | tf_op jit(solution)/shard_map/pallas_call | solution.py:120
  42.7 0.0 collective-permute-done.11.refs_5_
  42.7 0.6 %collective-permute-done.12.refs_6_ = f32[2,64,128]{2,1,0:T(8,128)S(1)} collective-permute-done((f32[2,64,128]{2,1,0:T(8,128)S(1)}, f32[2,64,128]{2,1,0:T(8,128)S(1)}, u32[]{:S(2)}, u32[]{:S(2)}) %collective-permute-start.12) | collective-permute-done | bytes 65568 | tf_op jit(solution)/shard_map/ppermute | solution.py:538
  43.3 0.0 collective-permute-done.9.refs_0_
  43.3 1.3 %shard_map.149 = (f32[2,64,512]{2,1,0:T(8,128)}, f32[2,64,512]{2,1,0:T(8,128)}) custom-call(f32[64,640]{1,0:T(8,128)S(1)} %collective-permute-done.9.refs_0_, f32[64,640]{1,0:T(8,128)S(1)} %get-tuple-element.41.refs_0_.refs_1_, bf16[512,512]{1,0:T(8,128)(2,1)S(1)} %get-tuple-element.42.refs_1_.refs_2_, f32[2,512]{1,0:T(2,128)S(1)} %get-tuple-element.43.refs_2_.refs_3_, ...), custom_call_target="tpu_custom_call" | custom-call | flops 268435456 | bytes 1048576 | tf_op jit(solution)/shard_map/pallas_call | solution.py:120
  (3 shorter events, 0.1 us)
Async XLA Ops:
  0.6 30.9 %copy-start = (f32[2,1,512,2,1,512]{5,4,3,2,1,0:T(1,128)S(1)}, f32[2,1,512,2,1,512]{5,4,3,2,1,0:T(1,128)}, u32[]{:S(2)}) copy-start(f32[2,1,512,2,1,512]{5,4,3,2,1,0:T(1,128)} %param.12) | copy-start | bytes 12582916
  0.6 7.2 %collective-permute-start = (f32[2,64,512]{2,1,0:T(8,128)}, f32[2,64,512]{2,1,0:T(8,128)S(1)}, u32[]{:S(2)}, u32[]{:S(2)}) collective-permute-start(f32[2,64,512]{2,1,0:T(8,128)} %bitcast.18), channel_id=1, source_target_pairs={{0,1},{1,0},{2,3},{3,2},{4,5},{5,4},{6,7},{7,6},{8,9},{9,8},{10,11... | collective-permute-start | bytes 786440 | tf_op jit(solution)/shard_map/ppermute | solution.py:538
  2.8 8.7 %collective-permute-start.3 = (f32[1,160,128]{2,1,0:T(8,128)S(1)}, f32[1,160,128]{2,1,0:T(8,128)S(1)}, u32[]{:S(2)}, u32[]{:S(2)}) collective-permute-start(f32[1,160,128]{2,1,0:T(8,128)S(1)} %get-tuple-element.32.refs_0_), channel_id=1, source_target_pairs={{0,4},{1,5},{2,6},{3,7},{4,0},{5,1},{6,2},{7,3},{8,12},{9,13},{10,... | collective-permute-start | bytes 245768 | tf_op jit(solution)/shard_map/ppermute | solution.py:541
  6.3 5.9 %collective-permute-start.7 = (f32[1,256,128]{2,1,0:T(8,128)S(1)}, f32[1,256,128]{2,1,0:T(8,128)S(1)}, u32[]{:S(2)}, u32[]{:S(2)}) collective-permute-start(f32[1,256,128]{2,1,0:T(8,128)S(1)} %get-tuple-element.37.refs_0_), channel_id=1, source_target_pairs={{0,16},{8,24},{16,0},{24,8},{1,17},{9,25},{17,1},{25,9},{2,18},{10... | collective-permute-start | bytes 393224 | tf_op jit(solution)/shard_map/ppermute | solution.py:544
  7.9 13.1 %collective-permute-start.1 = (f32[128,512]{1,0:T(8,128)S(1)}, f32[128,512]{1,0:T(8,128)S(1)}, u32[]{:S(2)}, u32[]{:S(2)}) collective-permute-start(f32[128,512]{1,0:T(8,128)S(1)} %shard_map.141.refs_1_.refs_6_), channel_id=1, source_target_pairs={{0,2},{1,3},{2,0},{3,1},{4,6},{5,7},{6,4},{7,5},{8,10},{9,11},{10,... | collective-permute-start | bytes 786440 | tf_op jit(solution)/shard_map/ppermute | solution.py:541
  11.5 8.9 %collective-permute-start.4 = (f32[2,160,128]{2,1,0:T(8,128)S(1)}, f32[2,160,128]{2,1,0:T(8,128)S(1)}, u32[]{:S(2)}, u32[]{:S(2)}) collective-permute-start(f32[2,160,128]{2,1,0:T(8,128)S(1)} %shard_map.143.refs_1_), channel_id=1, source_target_pairs={{0,2},{1,3},{2,0},{3,1},{4,6},{5,7},{6,4},{7,5},{8,10},{9,11},{10,... | collective-permute-start | bytes 491528 | tf_op jit(solution)/shard_map/ppermute | solution.py:541
  12.3 10.8 %collective-permute-start.8 = (f32[2,256,128]{2,1,0:T(8,128)S(1)}, f32[2,256,128]{2,1,0:T(8,128)S(1)}, u32[]{:S(2)}, u32[]{:S(2)}) collective-permute-start(f32[2,256,128]{2,1,0:T(8,128)S(1)} %shard_map.146.refs_1_), channel_id=1, source_target_pairs={{0,8},{8,0},{16,24},{24,16},{1,9},{9,1},{17,25},{25,17},{2,10},{10... | collective-permute-start | bytes 786440 | tf_op jit(solution)/shard_map/ppermute | solution.py:544
  13.8 8.2 %collective-permute-start.5 = (f32[2,160,128]{2,1,0:T(8,128)S(1)}, f32[2,160,128]{2,1,0:T(8,128)S(1)}, u32[]{:S(2)}, u32[]{:S(2)}) collective-permute-start(f32[2,160,128]{2,1,0:T(8,128)S(1)} %shard_map.143.refs_1_), channel_id=1, source_target_pairs={{0,1},{1,0},{2,3},{3,2},{4,5},{5,4},{6,7},{7,6},{8,9},{9,8},{10,11... | collective-permute-start | bytes 491528 | tf_op jit(solution)/shard_map/ppermute | solution.py:538
  20.3 1.7 %collective-permute-start.6 = (f32[2,160,128]{2,1,0:T(8,128)S(1)}, f32[2,160,128]{2,1,0:T(8,128)S(1)}, u32[]{:S(2)}, u32[]{:S(2)}) collective-permute-start(f32[2,160,128]{2,1,0:T(8,128)S(1)} %collective-permute-done.4.refs_2_), channel_id=1, source_target_pairs={{0,1},{1,0},{2,3},{3,2},{4,5},{5,4},{6,7},{7,6},{8,9},{9,8},{10,11... | collective-permute-start | bytes 491528 | tf_op jit(solution)/shard_map/ppermute | solution.py:538
  21.3 9.7 %collective-permute-start.2 = (f32[64,512]{1,0:T(8,128)S(1)}, f32[64,512]{1,0:T(8,128)S(1)}, u32[]{:S(2)}, u32[]{:S(2)}) collective-permute-start(f32[64,512]{1,0:T(8,128)S(1)} %shard_map.142.refs_0_), channel_id=1, source_target_pairs={{0,4},{1,5},{2,6},{3,7},{4,0},{5,1},{6,2},{7,3},{8,12},{9,13},{10,... | collective-permute-start | bytes 393224 | tf_op jit(solution)/shard_map/ppermute | solution.py:541
  36.3 7.0 %collective-permute-start.9 = (f32[64,640]{1,0:T(8,128)S(1)}, f32[64,640]{1,0:T(8,128)S(1)}, u32[]{:S(2)}, u32[]{:S(2)}) collective-permute-start(f32[64,640]{1,0:T(8,128)S(1)} %get-tuple-element.41.refs_0_.refs_1_), channel_id=1, source_target_pairs={{0,1},{1,0},{2,3},{3,2},{4,5},{5,4},{6,7},{7,6},{8,9},{9,8},{10,11... | collective-permute-start | bytes 491528 | tf_op jit(solution)/shard_map/ppermute | solution.py:538
  36.4 5.7 %collective-permute-start.10 = (f32[2,64,128]{2,1,0:T(8,128)S(1)}, f32[2,64,128]{2,1,0:T(8,128)S(1)}, u32[]{:S(2)}, u32[]{:S(2)}) collective-permute-start(f32[2,64,128]{2,1,0:T(8,128)S(1)} %get-tuple-element.44.refs_3_), channel_id=1, source_target_pairs={{0,4},{1,5},{2,6},{3,7},{4,0},{5,1},{6,2},{7,3},{8,12},{9,13},{10,... | collective-permute-start | bytes 196616 | tf_op jit(solution)/shard_map/ppermute | solution.py:541
  36.5 6.2 %collective-permute-start.11 = (f32[2,64,128]{2,1,0:T(8,128)S(1)}, f32[2,64,128]{2,1,0:T(8,128)S(1)}, u32[]{:S(2)}, u32[]{:S(2)}) collective-permute-start(f32[2,64,128]{2,1,0:T(8,128)S(1)} %get-tuple-element.44.refs_3_), channel_id=1, source_target_pairs={{0,1},{1,0},{2,3},{3,2},{4,5},{5,4},{6,7},{7,6},{8,9},{9,8},{10,11... | collective-permute-start | bytes 196616 | tf_op jit(solution)/shard_map/ppermute | solution.py:538
  42.1 1.3 %collective-permute-start.12 = (f32[2,64,128]{2,1,0:T(8,128)S(1)}, f32[2,64,128]{2,1,0:T(8,128)S(1)}, u32[]{:S(2)}, u32[]{:S(2)}) collective-permute-start(f32[2,64,128]{2,1,0:T(8,128)S(1)} %collective-permute-done.10.refs_4_), channel_id=1, source_target_pairs={{0,1},{1,0},{2,3},{3,2},{4,5},{5,4},{6,7},{7,6},{8,9},{9,8},{10,11... | collective-permute-start | bytes 196616 | tf_op jit(solution)/shard_map/ppermute | solution.py:538
